TPU v7x, 128 devices: a whole 4x4x4 slice. The times are simulated.
128 devices in a mesh: wave: 32 (over x, y, core), lev: 4 (over z).
Axes of the slice: x: 4, y: 4, z: 4, core: 2. Of those that a mesh axis runs over, the one named last changes fastest.
Arguments:
- coefficients: bfloat16 [640, 640, 512], P('wave', 'lev'), may hold values from -6 to 6
- factors: bfloat16 [5, 2, 640, 20, 640], P(None, None, 'wave', None, 'lev'), may hold values from -1 to 1
- wave_ids: int32 [640], replicated, may hold values from 0 to 639, each once
Outputs:
- grid: bfloat16 [640, 256, 2560], P(('wave', 'lev'))
Inputs may be any that keep to these rules, and one draw needn't show every extreme that they name: `wave_ids`: each wavenumber 0 .. 639 appears exactly once.
All inputs are finite; a program needn't handle non-finite values.
Results may differ from a plain program's by a relative error of at most 0.0079.
Values may be sent and summed in bfloat16 or wider, within the bound.
No kernel may reach another device: no remote copies, remote signals or barrier semaphores. Data moves between devices by JAX's collectives and lax.ppermute only.
A program may use at most 64 MiB of HBM per device.

v0:
```python
import math

import jax
import jax.numpy as jnp
from jax import lax
from jax.sharding import PartitionSpec as P

NLON = 2560


def swapped(block, axis, apart):
    count = lax.axis_size(axis)
    route = []
    for low in range(count):
        high = low | 1 << apart
        if high != low and high < count:
            route += [(low, high), (high, low)]
    return lax.ppermute(block, axis, route)


def body(coefficients, factors, wave_ids):
    wave_count = lax.axis_size("wave")
    sections = wave_count.bit_length() - 1
    deg_block = coefficients.shape[0]
    wave_block = coefficients.shape[1]
    channels = coefficients.shape[2]
    total_waves = wave_ids.shape[0]
    wave_pos = lax.axis_index("wave")
    lev_pos = lax.axis_index("lev")
    own_ids = lax.dynamic_slice_in_dim(wave_ids, lev_pos * wave_block, wave_block, 0)
    degree = wave_pos * deg_block + jnp.arange(deg_block, dtype=jnp.int32)
    live_mask = (degree[:, None] >= own_ids[None, :])[:, :, None]
    current = jnp.where(live_mask, coefficients, jnp.zeros((), coefficients.dtype))
    for section in range(sections):
        partner = swapped(current, "wave", section)
        combined = jnp.einsum(
            "oim,imc->omc", factors[section, 0], current, preferred_element_type=jnp.float32
        )
        combined = combined + jnp.einsum(
            "oim,imc->omc", factors[section, 1], partner, preferred_element_type=jnp.float32
        )
        current = combined.astype(jnp.bfloat16)
    grid_rows = lax.all_to_all(current, "lev", split_axis=0, concat_axis=1, tiled=True)
    longitude = jnp.arange(NLON, dtype=jnp.int32)
    phases = wave_ids[:, None] * longitude[None, :] % NLON
    angles = phases.astype(jnp.float32) * (2.0 * math.pi / NLON)
    weight = jnp.where(wave_ids == 0, 1.0, 2.0).astype(jnp.float32) / math.sqrt(2.0 * total_waves)
    cosine_part = weight[:, None] * jnp.cos(angles)
    sine_part = -weight[:, None] * jnp.sin(angles)
    fourier_table = jnp.stack([cosine_part, sine_part], axis=1).astype(jnp.bfloat16)
    lat_count = grid_rows.shape[0]
    split_rows = grid_rows.reshape(lat_count, total_waves, 2, channels // 2)
    synthesized = jnp.einsum(
        "rmpc,mpj->rcj", split_rows, fourier_table, preferred_element_type=jnp.float32
    )
    return synthesized.astype(jnp.bfloat16)


def solution(mesh):
    in_specs = (P("wave", "lev", None), P(None, None, "wave", None, "lev"), P())
    out_specs = P(("wave", "lev"), None, None)
    return jax.shard_map(body, mesh=mesh, in_specs=in_specs, out_specs=out_specs, check_vma=False)
```

profile of v0, /device:TPU:1, one launch (start us, length us, event | category | flops | bytes accessed | tf_op | source)
XLA Modules:
  0.0 413.9 jit_solution(2084151253647331986)
XLA Ops:
  0.0 0.0 copy-start.4
  0.0 0.9 dynamic_slice.3
  0.9 0.1 broadcast_compare_fusion
  1.0 2.2 broadcast_select_fusion
  3.2 1.5 collective-permute-start
  4.7 0.0 copy-done.4
  4.7 4.6 %fusion.50 = (bf16[1,1,20,20,160]{4,1,3,2,0:T(2,128)(2,1)}, bf16[1,1,20,20,160]{4,1,3,2,0:T(2,128)(2,1)}, bf16[1,1,20,20,160]{4,1,3,2,0:T(2,128)(2,1)}, bf16[1,1...) fusion(bf16[5,2,20,20,160]{4,1,3,2,0:T(2,128)(2,1)S(1)} %copy-d, ...), kind=kLoop, calls=%fused_computation.55 | loop fusion | bytes 2560000 | tf_op jit(solution)/shard_map/slice | solution.py:40
  9.3 3.1 copy.56
  12.4 3.1 copy.57
  15.5 0.0 copy-start.9
  15.5 3.4 fusion.22
  18.9 0.0 collective-permute-done
  18.9 0.0 copy-done.9
  18.9 5.0 %fusion.7 = bf16[20,160,512]{2,0,1:T(8,128)(2,1)S(1)} fusion(f32[160,512,20]{1,2,0:T(8,128)S(1)} %fusion.22, bf16[20,160,512]{2,1,0:T(8,128)(2,1)} %collective-permute-done, bf16[1,1,20,20,160]{3,2,4,1,0:T(8,128)(2,1)S(1)} %copy-done.9), kind=kOutput, calls=%fused_computation.18 | convolution fusion | flops 68812800 | bytes 13235200 | tf_op jit(solution)/shard_map/oim,imc->omc/dot_general | solution.py:39
  24.0 0.0 copy-start.1
  24.0 1.9 copy-done.1
  25.9 2.8 copy.35
  28.7 1.4 collective-permute-start.1
  30.1 3.1 copy.58
  33.2 3.1 copy.59
  36.3 0.0 copy-start.5
  36.3 3.6 fusion.44
  40.0 61.5 %collective-permute-done.1 = bf16[20,160,512]{2,1,0:T(8,128)(2,1)S(1)} collective-permute-done((bf16[20,160,512]{2,1,0:T(8,128)(2,1)}, bf16[20,160,512]{2,1,0:T(8,128)(2,1)S(1)}, u32[]{:S(2)}, u32[]{:S(2)}) %collective-permute-start.1) | collective-permute-done | bytes 3276832 | tf_op jit(solution)/shard_map/ppermute | solution.py:18
  101.4 0.0 copy-done.5
  101.4 3.1 fusion.8
  104.5 0.0 copy-start.2
  104.5 1.9 copy-done.2
  106.4 2.8 copy.39
  109.2 3.0 collective-permute-start.2
  112.2 3.1 copy.60
  115.3 3.1 copy.61
  118.5 3.6 fusion.41
  122.1 60.5 %collective-permute-done.2 = bf16[20,160,512]{2,1,0:T(8,128)(2,1)S(1)} collective-permute-done((bf16[20,160,512]{2,1,0:T(8,128)(2,1)}, bf16[20,160,512]{2,1,0:T(8,128)(2,1)S(1)}, u32[]{:S(2)}, u32[]{:S(2)}) %collective-permute-start.2) | collective-permute-done | bytes 3276832 | tf_op jit(solution)/shard_map/ppermute | solution.py:18
  182.6 0.0 copy-done.6
  182.6 3.1 fusion.9
  185.7 0.0 copy-start.3
  185.7 1.9 copy-done.3
  187.6 2.8 copy.43
  190.4 1.2 collective-permute-start.3
  191.7 3.1 copy.62
  194.8 3.1 copy.63
  197.9 3.6 fusion.38
  201.6 59.8 %collective-permute-done.3 = bf16[20,160,512]{2,1,0:T(8,128)(2,1)S(1)} collective-permute-done((bf16[20,160,512]{2,1,0:T(8,128)(2,1)}, bf16[20,160,512]{2,1,0:T(8,128)(2,1)S(1)}, u32[]{:S(2)}, u32[]{:S(2)}) %collective-permute-start.3) | collective-permute-done | bytes 3276832 | tf_op jit(solution)/shard_map/ppermute | solution.py:18
  261.4 0.0 copy-done.7
  261.4 3.1 fusion.10
  264.4 0.0 copy-start
  264.5 1.9 copy-done
  266.4 2.8 copy.47
  269.2 2.7 collective-permute-start.4
  271.9 3.1 copy.64
  275.0 3.1 copy.65
  278.1 3.6 fusion.35
  281.8 58.9 %collective-permute-done.4 = bf16[20,160,512]{2,1,0:T(8,128)(2,1)S(1)} collective-permute-done((bf16[20,160,512]{2,1,0:T(8,128)(2,1)}, bf16[20,160,512]{2,1,0:T(8,128)(2,1)S(1)}, u32[]{:S(2)}, u32[]{:S(2)}) %collective-permute-start.4) | collective-permute-done | bytes 3276832 | tf_op jit(solution)/shard_map/ppermute | solution.py:18
  340.7 0.0 copy-done.8
  340.7 3.1 fusion.11
  343.8 2.8 copy.50
  346.6 5.1 %all-to-all-start = ((bf16[20,160,512]{2,1,0:T(8,128)(2,1)}), bf16[20,160,512]{2,1,0:T(8,128)(2,1)S(1)}, u32[]{:S(2)}, u32[]{:S(2)}) async-start(bf16[20,160,512]{2,1,0:T(8,128)(2,1)} %copy.50), calls=%async_computation | async-start | bytes 6553600 | tf_op jit(solution)/shard_map/all_to_all | solution.py:43
  351.7 0.0 copy-done.11
  351.8 29.7 %multiply_convert_fusion.1 = (bf16[640,1,2560]{2,0,1:T(8,128)(2,1)}, bf16[640,1,2560]{2,0,1:T(8,128)(2,1)}) fusion(s32[640]{0:T(1024)S(1)} %copy-done.11, f32[640]{0:T(1024)S(1)} %get-tuple-element.17, f32[640]{0:T(1024)S(1)} %get-tuple-element.18), kind=kLoop, calls=%fused_computation.13 | loop fusion | flops 21299200 | bytes 6561280 | tf_op jit(solution)/shard_map/convert
  381.5 5.5 %all-to-all-done = bf16[20,160,512]{2,1,0:T(8,128)(2,1)S(1)} async-done(((bf16[20,160,512]{2,1,0:T(8,128)(2,1)}), bf16[20,160,512]{2,1,0:T(8,128)(2,1)S(1)}, u32[]{:S(2)}, u32[]{:S(2)}) %all-to-all-start) | async-done | bytes 3276832 | tf_op jit(solution)/shard_map/all_to_all | solution.py:43
  386.9 5.7 %copy.54 = bf16[5,4,160,512]{2,1,3,0:T(4,128)(2,1)} copy(bf16[5,4,160,512]{3,2,0,1:T(8,128)(2,1)S(1)} %bitcast.56) | data formatting | bytes 6553600 | tf_op jit(solution)/shard_map/reshape | solution.py:52
  392.6 8.3 %reshape.156 = bf16[5,640,2,256]{1,3,2,0:T(8,128)(2,1)} reshape(bf16[5,4,160,512]{2,1,3,0:T(4,128)(2,1)} %copy.54) | data formatting | bytes 6553600 | tf_op jit(solution)/shard_map/reshape | solution.py:52
  400.9 0.0 copy-done.10
  400.9 12.9 %bitcast_convert_fusion = bf16[5,256,2560]{2,1,0:T(8,128)(2,1)} fusion(bf16[5,640,2,256]{1,3,2,0:T(8,128)(2,1)} %reshape.156, bf16[640,1,2560]{2,0,1:T(8,128)(2,1)} %get-tuple-element.16, bf16[640,1,2560]{2,0,1:T(8,128)(2,1)S(1)} %copy-done.10), kind=kOutput, calls=%fused_computation | convolution fusion | flops 8395161600 | bytes 16384000 | tf_op jit(solution)/shard_map/rmpc,mpj->rcj/dot_general | solution.py:53
  (7 shorter events, 0.0 us)
Async XLA Ops:
  0.0 4.7 %copy-start.4 = (bf16[5,2,20,20,160]{4,1,3,2,0:T(2,128)(2,1)S(1)}, bf16[5,2,20,20,160]{4,1,3,2,0:T(2,128)(2,1)}, u32[]{:S(2)}) copy-start(bf16[5,2,20,20,160]{4,1,3,2,0:T(2,128)(2,1)} %param.4) | copy-start | bytes 3840004
  3.2 15.7 %collective-permute-start = (bf16[20,160,512]{2,1,0:T(8,128)(2,1)S(1)}, bf16[20,160,512]{2,1,0:T(8,128)(2,1)}, u32[]{:S(2)}, u32[]{:S(2)}) collective-permute-start(bf16[20,160,512]{2,1,0:T(8,128)(2,1)S(1)} %broadcast_select_fusion), channel_id=1, source_target_pairs={{0,4},{4,0},{8,12},{12,8},{16,20},{20,16},{24,28},{28,24},{32,36},... | collective-permute-start | bytes 9830408 | tf_op jit(solution)/shard_map/ppermute | solution.py:18
  15.5 3.4 copy-start.9
  24.0 1.9 copy-start.1
  28.7 72.7 %collective-permute-start.1 = (bf16[20,160,512]{2,1,0:T(8,128)(2,1)}, bf16[20,160,512]{2,1,0:T(8,128)(2,1)S(1)}, u32[]{:S(2)}, u32[]{:S(2)}) collective-permute-start(bf16[20,160,512]{2,1,0:T(8,128)(2,1)} %copy.35), channel_id=1, source_target_pairs={{0,8},{8,0},{4,12},{12,4},{16,24},{24,16},{20,28},{28,20},{32,40},... | collective-permute-start | bytes 9830408 | tf_op jit(solution)/shard_map/ppermute | solution.py:18
  36.3 65.1 %copy-start.5 = (bf16[1,1,20,20,160]{3,2,4,1,0:T(8,128)(2,1)S(1)}, bf16[1,1,20,20,160]{3,2,4,1,0:T(8,128)(2,1)}, u32[]{:S(2)}) copy-start(bf16[1,1,20,20,160]{3,2,4,1,0:T(8,128)(2,1)} %copy.59) | copy-start | bytes 384004
  104.5 1.9 copy-start.2
  109.2 73.4 %collective-permute-start.2 = (bf16[20,160,512]{2,1,0:T(8,128)(2,1)}, bf16[20,160,512]{2,1,0:T(8,128)(2,1)S(1)}, u32[]{:S(2)}, u32[]{:S(2)}) collective-permute-start(bf16[20,160,512]{2,1,0:T(8,128)(2,1)} %copy.39), channel_id=1, source_target_pairs={{0,16},{16,0},{4,20},{20,4},{8,24},{24,8},{12,28},{28,12},{32,48},... | collective-permute-start | bytes 9830408 | tf_op jit(solution)/shard_map/ppermute | solution.py:18
  118.5 64.1 %copy-start.6 = (bf16[1,1,20,20,160]{3,2,4,1,0:T(8,128)(2,1)S(1)}, bf16[1,1,20,20,160]{3,2,4,1,0:T(8,128)(2,1)}, u32[]{:S(2)}) copy-start(bf16[1,1,20,20,160]{3,2,4,1,0:T(8,128)(2,1)} %copy.61) | copy-start | bytes 384004
  185.7 1.9 copy-start.3
  190.4 70.9 %collective-permute-start.3 = (bf16[20,160,512]{2,1,0:T(8,128)(2,1)}, bf16[20,160,512]{2,1,0:T(8,128)(2,1)S(1)}, u32[]{:S(2)}, u32[]{:S(2)}) collective-permute-start(bf16[20,160,512]{2,1,0:T(8,128)(2,1)} %copy.43), channel_id=1, source_target_pairs={{0,32},{32,0},{4,36},{36,4},{8,40},{40,8},{12,44},{44,12},{16,48},... | collective-permute-start | bytes 9830408 | tf_op jit(solution)/shard_map/ppermute | solution.py:18
  197.9 63.4 %copy-start.7 = (bf16[1,1,20,20,160]{3,2,4,1,0:T(8,128)(2,1)S(1)}, bf16[1,1,20,20,160]{3,2,4,1,0:T(8,128)(2,1)}, u32[]{:S(2)}) copy-start(bf16[1,1,20,20,160]{3,2,4,1,0:T(8,128)(2,1)} %copy.63) | copy-start | bytes 384004
  264.4 1.9 copy-start
  269.2 71.5 %collective-permute-start.4 = (bf16[20,160,512]{2,1,0:T(8,128)(2,1)}, bf16[20,160,512]{2,1,0:T(8,128)(2,1)S(1)}, u32[]{:S(2)}, u32[]{:S(2)}) collective-permute-start(bf16[20,160,512]{2,1,0:T(8,128)(2,1)} %copy.47), channel_id=1, source_target_pairs={{0,64},{64,0},{4,68},{68,4},{8,72},{72,8},{12,76},{76,12},{16,80},... | collective-permute-start | bytes 9830408 | tf_op jit(solution)/shard_map/ppermute | solution.py:18
  278.1 62.6 %copy-start.8 = (bf16[1,1,20,20,160]{3,2,4,1,0:T(8,128)(2,1)S(1)}, bf16[1,1,20,20,160]{3,2,4,1,0:T(8,128)(2,1)}, u32[]{:S(2)}) copy-start(bf16[1,1,20,20,160]{3,2,4,1,0:T(8,128)(2,1)} %copy.65) | copy-start | bytes 384004
  346.6 5.1 %copy-start.11 = (s32[640]{0:T(1024)S(1)}, s32[640]{0:T(1024)}, u32[]{:S(2)}) copy-start(s32[640]{0:T(1024)} %param.5) | copy-start | bytes 7684
  346.6 40.3 %all-to-all-start = ((bf16[20,160,512]{2,1,0:T(8,128)(2,1)}), bf16[20,160,512]{2,1,0:T(8,128)(2,1)S(1)}, u32[]{:S(2)}, u32[]{:S(2)}) async-start(bf16[20,160,512]{2,1,0:T(8,128)(2,1)} %copy.50), calls=%async_computation | async-start | bytes 6553600 | tf_op jit(solution)/shard_map/all_to_all | solution.py:43
  392.6 8.3 %copy-start.10 = (bf16[640,1,2560]{2,0,1:T(8,128)(2,1)S(1)}, bf16[640,1,2560]{2,0,1:T(8,128)(2,1)}, u32[]{:S(2)}) copy-start(bf16[640,1,2560]{2,0,1:T(8,128)(2,1)} %get-tuple-element.15) | copy-start | bytes 9830404
where the time goes:
time: 418 us; the launch traced here: 414 us
  waiting for transfers between devices  246 us (59%)
  local copies, waits for them, and re-layouts  72.5 us (17%)
  matrix products  48.1 us (12%)
  other arithmetic  32 us (8%)
  starting transfers between devices  15 us (4%)
    ppermute x5, waiting for transfers between devices, swapped(): return lax.ppermute(block, axis, route)  241 us
    unnamed x34, local copies, waits for them, and re-layouts  39 us
    another operation x1, other arithmetic  29.7 us
    dot_general x5, matrix products, body(): jnp.einsum('oim,imc->omc', factors[section, 0], current, preferred_elemen...  17.9 us
    dot_general x5, matrix products, body(): jnp.einsum('oim,imc->omc', factors[section, 1], partner, preferred_elemen...  17.3 us
    convert_element_type x5, local copies, waits for them, and re-layouts, body(): current = combined.astype(jnp.bfloat16)  14 us
    reshape x2, local copies, waits for them, and re-layouts, body(): split_rows = grid_rows.reshape(lat_count, total_waves, 2, channels // 2)  14 us
    dot_general x1, matrix products, body(): jnp.einsum('rmpc,mpj->rcj', split_rows, fourier_table, preferred_element_...  12.9 us
  transfers between devices with their start and end apart: 6, of which 5 were waited for; matrix products, arithmetic and copies ran while one was open for 20% of the time, Pallas kernels for 0%

commit v1 on v0

v1 whole, which is shorter than its diff:
```python
import math

import jax
import jax.numpy as jnp
import numpy as np
from jax import lax
from jax.experimental import pallas as pl
from jax.experimental.pallas import tpu as pltpu
from jax.sharding import PartitionSpec as P

NLON = 2560
SECTIONS = 5
BLOCKS = 32
BANDS = 4
DEG = 20
OWN = 5
CH = 512
HALF = 256
ROWS = DEG * OWN
PADR = 112
SLOT = 56


def select_matrices():
    q = lax.broadcasted_iota(jnp.int32, (SECTIONS, 2, 256, 256), 2)
    lane = lax.broadcasted_iota(jnp.int32, (SECTIONS, 2, 256, 256), 3)
    s = lax.broadcasted_iota(jnp.int32, (SECTIONS, 2, 256, 256), 0)
    v = lax.broadcasted_iota(jnp.int32, (SECTIONS, 2, 256, 256), 1)
    part = (lane // 128) ^ v
    inner = lane % 128
    hit = (q == s * 40 + (inner % DEG) * 2 + part) & (inner < ROWS)
    return hit.astype(jnp.bfloat16)


def diagonal_mask():
    row = lax.broadcasted_iota(jnp.int32, (PADR, 256), 0)
    inner = lax.broadcasted_iota(jnp.int32, (PADR, 256), 1) % 128
    hit = (row // DEG == inner // DEG) & (row < ROWS) & (inner < ROWS)
    return hit.astype(jnp.float32)


def send_order():
    row = lax.broadcasted_iota(jnp.int32, (BANDS * SLOT, 256), 0)
    col = lax.broadcasted_iota(jnp.int32, (BANDS * SLOT, 256), 1)
    band, inner = row // SLOT, row % SLOT
    part, kr = inner // 25, inner % 25
    want = part * 128 + (kr // 5) * DEG + 5 * band + kr % 5
    return ((col == want) & (inner < 50)).astype(jnp.bfloat16)


def receive_order():
    row = lax.broadcasted_iota(jnp.int32, (400, 8 * SLOT), 0)
    col = lax.broadcasted_iota(jnp.int32, (400, 8 * SLOT), 1)
    part, lat = row // 200, (row // 40) % 5
    src, k = (row % 40) // 5, row % 5
    return (col == src * SLOT + part * 25 + k * 5 + lat).astype(jnp.bfloat16)


def butterfly_kernel(rx_ref, e_ref, mask_ref, first_ref, order_ref, out_ref, xa, xb, fc):
    zeros_x = jnp.zeros((32, CH), jnp.bfloat16)
    zeros_f = jnp.zeros((16, 256), jnp.bfloat16)

    def load(b, carry):
        xa[b, pl.ds(96, 32), :] = zeros_x
        xb[b, pl.ds(96, 32), :] = zeros_x
        fc[b, pl.ds(96, 16), :] = zeros_f
        xa[b, pl.ds(0, ROWS), :] = rx_ref[b, :, :CH]
        fc[b, pl.ds(0, ROWS), :] = rx_ref[b, :, CH:]
        return carry

    lax.fori_loop(0, BLOCKS, load, 0)
    lane_high = lax.broadcasted_iota(jnp.int32, (8, 256), 1) // 128
    bufs = (xa, xb)
    for s in range(SECTIONS):
        src, dst = bufs[s % 2], bufs[(s + 1) % 2]

        def pair(j, carry, s=s, src=src, dst=dst):
            low = (j >> s) * (2 << s) + (j & ((1 << s) - 1))
            high = low + (1 << s)
            mask = mask_ref[...]
            if s == 0:
                start = DEG * (low + lane_high * (1 << s))
                live = (start >= first_ref[...]).astype(jnp.float32)
                mask = mask * live[0:1, :]
            f_low = jnp.dot(fc[low], e_ref[s, 0], preferred_element_type=jnp.float32) * mask
            f_high = jnp.dot(fc[high], e_ref[s, 1], preferred_element_type=jnp.float32) * mask
            left = jnp.concatenate([f_low.astype(jnp.bfloat16), f_high.astype(jnp.bfloat16)], axis=0)
            right = jnp.concatenate([src[low], src[high]], axis=0)
            y = jnp.dot(left, right, preferred_element_type=jnp.float32).astype(jnp.bfloat16)
            dst[low, pl.ds(0, PADR), :] = y[:PADR]
            dst[high, pl.ds(0, PADR), :] = y[PADR:]
            return carry

        lax.fori_loop(0, BLOCKS // 2, pair, 0, unroll=2)
    last = bufs[SECTIONS % 2]

    def emit(b, carry):
        right = jnp.concatenate([last[b, :, :HALF], last[b, :, HALF:]], axis=0)
        y = jnp.dot(order_ref[...], right, preferred_element_type=jnp.float32)
        for band in range(BANDS):
            out_ref[BANDS * b + band] = y[band * SLOT:(band + 1) * SLOT].astype(jnp.bfloat16)
        return carry

    lax.fori_loop(0, BLOCKS, emit, 0, unroll=2)


def butterfly(rx, first):
    return pl.pallas_call(
        butterfly_kernel,
        out_shape=jax.ShapeDtypeStruct((BLOCKS * BANDS, SLOT, HALF), jnp.bfloat16),
        scratch_shapes=[
            pltpu.VMEM((BLOCKS, 128, CH), jnp.bfloat16),
            pltpu.VMEM((BLOCKS, 128, CH), jnp.bfloat16),
            pltpu.VMEM((BLOCKS, PADR, 256), jnp.bfloat16),
        ],
        compiler_params=pltpu.CompilerParams(vmem_limit_bytes=60 << 20),
        name="butterfly",
    )(rx, select_matrices(), diagonal_mask(), first, send_order())


def fourier_kernel(u_ref, order_ref, table_ref, out_ref, v):
    @pl.when(pl.program_id(0) == 0)
    def _():
        for g in range(16):
            piece = u_ref[pl.ds(8 * g, 8)].reshape(8 * SLOT, HALF)
            y = jnp.dot(order_ref[...], piece, preferred_element_type=jnp.float32)
            for p in range(2):
                for r in range(5):
                    at = p * 200 + r * 40
                    v[r, pl.ds(p * 640 + 40 * g, 40), :] = y[at:at + 40].astype(jnp.bfloat16)

    for r in range(5):
        y = lax.dot_general(v[r], table_ref[...], (((0,), (0,)), ((), ())), preferred_element_type=jnp.float32)
        out_ref[r] = y.astype(jnp.bfloat16)


def fourier(u, table):
    tile = 256
    return pl.pallas_call(
        fourier_kernel,
        out_shape=jax.ShapeDtypeStruct((5, HALF, NLON), jnp.bfloat16),
        grid=(NLON // tile,),
        in_specs=[
            pl.BlockSpec((BLOCKS * BANDS, SLOT, HALF), lambda j: (0, 0, 0)),
            pl.BlockSpec((400, 8 * SLOT), lambda j: (0, 0)),
            pl.BlockSpec((1280, tile), lambda j: (0, j)),
        ],
        out_specs=pl.BlockSpec((5, HALF, tile), lambda j: (0, 0, j)),
        scratch_shapes=[pltpu.VMEM((5, 1280, HALF), jnp.bfloat16)],
        compiler_params=pltpu.CompilerParams(vmem_limit_bytes=60 << 20),
        name="fourier",
    )(u, receive_order(), table)


def fourier_table(ids):
    longitude = jnp.arange(NLON, dtype=jnp.int32)
    phases = ids[:, None] * longitude[None, :] % NLON
    angles = phases.astype(jnp.float32) * (2.0 * math.pi / NLON)
    weight = jnp.where(ids == 0, 1.0, 2.0).astype(jnp.float32) / math.sqrt(2.0 * ids.shape[0])
    cosine_part = weight[:, None] * jnp.cos(angles)
    sine_part = -weight[:, None] * jnp.sin(angles)
    return jnp.concatenate([cosine_part, sine_part], axis=0).astype(jnp.bfloat16)


def body(coefficients, factors, wave_ids):
    wave_pos = lax.axis_index("wave")
    lev_pos = lax.axis_index("lev")
    flat = factors.transpose(2, 4, 0, 3, 1).reshape(DEG, OWN * BLOCKS, 200)
    flat = jnp.pad(flat, ((0, 0), (0, 0), (0, 56)))
    joined = jnp.concatenate([coefficients, flat], axis=2)
    send = joined.reshape(DEG, BLOCKS, OWN, 768).transpose(1, 2, 0, 3).reshape(BLOCKS, ROWS, 768)
    rx = lax.all_to_all(send, "wave", 0, 0, tiled=True)
    own_ids = lax.dynamic_slice_in_dim(wave_ids, lev_pos * (OWN * BLOCKS) + wave_pos * OWN, OWN, 0)
    first = (own_ids[:, None] - jnp.arange(DEG, dtype=jnp.int32)[None, :]).reshape(ROWS)
    first = jnp.pad(first, (0, 28))
    first = jnp.broadcast_to(jnp.concatenate([first, first])[None, :], (8, 256))
    rows = butterfly(rx, first)
    u = lax.all_to_all(rows, ("wave", "lev"), 0, 0, tiled=True)
    ids = wave_ids.reshape(BANDS, BLOCKS, OWN).transpose(1, 0, 2).reshape(-1)
    return fourier(u, fourier_table(ids))


def solution(mesh):
    in_specs = (P("wave", "lev", None), P(None, None, "wave", None, "lev"), P())
    out_specs = P(("wave", "lev"), None, None)
    return jax.shard_map(body, mesh=mesh, in_specs=in_specs, out_specs=out_specs, check_vma=False)
```

time: 418 us -> 204 us (0.49)
  waiting for transfers between devices: 246 us -> 72.2 us
  local copies, waits for them, and re-layouts: 72.5 us -> 21.8 us
  matrix products: 48.1 us -> 0 us
  Pallas kernels: 0 us -> 47.3 us
  other arithmetic: 32 us -> 40.5 us
  starting transfers between devices: 15 us -> 21.8 us
    ppermute x5 -> x0, waiting for transfers between devices: 241 us -> none  [swapped(): return lax.ppermute(block, axis, route)]
    all_to_all x1 -> x2, waiting for transfers between devices: 5.46 us -> 72.2 us  [the longest x1 59.6 us: body(): rx = lax.all_to_all(send, 'wave', 0, 0, tiled=True)]
    dot_general x11 -> x0, matrix products: 48.1 us -> none  [the longest x5 17.9 us: body(): jnp.einsum('oim,imc->omc', factors[section, 0], current, preferred_elemen...]
    pallas_call x0 -> x2, Pallas kernels: none -> 47.3 us  [the longest x1 30.3 us: butterfly(): pl.pallas_call(butterfly_kernel, out_shape=jax.ShapeDtypeStruct((BLOCKS *...]
    unnamed x34 -> x3, local copies, waits for them, and re-layouts: 39 us -> 2.82 us
    all_to_all x1 -> x2, starting transfers between devices: 5.14 us -> 21.8 us  [the longest x1 13 us: body(): u = lax.all_to_all(rows, ('wave', 'lev'), 0, 0, tiled=True)]
    convert_element_type x5 -> x0, local copies, waits for them, and re-layouts: 14 us -> none  [body(): current = combined.astype(jnp.bfloat16)]
    ppermute x5 -> x0, starting transfers between devices: 9.81 us -> none  [swapped(): return lax.ppermute(block, axis, route)]
  transfers between devices with their start and end apart: 6 -> 2, of which waited for: 5 -> 2; matrix products, arithmetic and copies ran while one was open for 20% -> 19% of each run, Pallas kernels for 0% -> 0%
where the time goes in v1:
time: 204 us
  waiting for transfers between devices  72.2 us (35%)
  Pallas kernels  47.3 us (23%)
  other arithmetic  40.5 us (20%)
  local copies, waits for them, and re-layouts  21.8 us (11%)
  starting transfers between devices  21.8 us (11%)
    all_to_all x1, waiting for transfers between devices, body(): rx = lax.all_to_all(send, 'wave', 0, 0, tiled=True)  59.6 us
    pallas_call x1, Pallas kernels, butterfly(): pl.pallas_call(butterfly_kernel, out_shape=jax.ShapeDtypeStruct((BLOCKS *...  30.3 us
    another operation x1, other arithmetic  28.5 us
    pallas_call x1, Pallas kernels, fourier(): pl.pallas_call(fourier_kernel, out_shape=jax.ShapeDtypeStruct((5, HALF, N...  17 us
    all_to_all x1, starting transfers between devices, body(): u = lax.all_to_all(rows, ('wave', 'lev'), 0, 0, tiled=True)  13 us
    all_to_all x1, waiting for transfers between devices, body(): u = lax.all_to_all(rows, ('wave', 'lev'), 0, 0, tiled=True)  12.6 us
    all_to_all x1, starting transfers between devices, body(): rx = lax.all_to_all(send, 'wave', 0, 0, tiled=True)  8.78 us
    reshape x1, local copies, waits for them, and re-layouts, body(): joined.reshape(DEG, BLOCKS, OWN, 768).transpose(1, 2, 0, 3)  5.1 us
  transfers between devices with their start and end apart: 2, of which 2 were waited for; matrix products, arithmetic and copies ran while one was open for 19% of the time, Pallas kernels for 0%

profile of v1, /device:TPU:1, one launch (start us, length us, event | category | flops | bytes accessed | tf_op | source)
XLA Modules:
  0.0 203.9 jit_solution(12797872467414140838)
XLA Ops:
  0.0 4.3 %copy.5 = bf16[20,160,5,20,2]{1,4,3,2,0:T(2,128)(2,1)} copy(bf16[20,160,5,20,2]{1,4,3,0,2:T(2,128)(2,1)} %bitcast.10) | data formatting | bytes 2560000 | tf_op jit(solution)/shard_map/transpose | solution.py:168
  4.3 4.4 %reshape.34 = bf16[20,160,200]{1,2,0:T(8,128)(2,1)S(1)} reshape(bf16[20,160,5,20,2]{1,4,3,2,0:T(2,128)(2,1)} %copy.5) | data formatting | bytes 2560000 | tf_op jit(solution)/shard_map/reshape | solution.py:168
  8.7 2.8 %copy.11 = bf16[20,160,200]{2,1,0:T(8,128)(2,1)} copy(bf16[20,160,200]{1,2,0:T(8,128)(2,1)S(1)} %reshape.34) | data formatting | bytes 2560000
  11.5 3.0 %fusion.6 = bf16[20,160,768]{2,1,0:T(8,128)(2,1)S(1)} fusion(bf16[20,160,200]{2,1,0:T(8,128)(2,1)} %copy.11, bf16[20,160,512]{2,1,0:T(8,128)(2,1)} %param.3), kind=kLoop, calls=%fused_computation.12 | loop fusion | flops 14745600 | bytes 9472000 | tf_op jit(solution)/shard_map/concatenate | solution.py:170
  14.5 2.9 %copy.7 = bf16[20,160,768]{2,0,1:T(8,128)(2,1)S(1)} copy(bf16[20,160,768]{2,1,0:T(8,128)(2,1)S(1)} %fusion.6) | data formatting | bytes 9830400 | tf_op jit(solution)/shard_map/concatenate | solution.py:170
  17.4 1.2 copy.8
  18.6 5.1 %copy.9 = bf16[32,100,768]{2,1,0:T(8,128)(2,1)} copy(bf16[32,100,768]{2,0,1:T(8,128)(2,1)S(1)} %bitcast.9) | data formatting | bytes 9830400 | tf_op jit(solution)/shard_map/reshape | solution.py:171
  23.7 0.0 copy-start
  23.7 8.8 %all-to-all-start = ((bf16[32,100,768]{2,1,0:T(8,128)(2,1)}), bf16[32,100,768]{2,1,0:T(8,128)(2,1)}, u32[]{:S(2)}, u32[]{:S(2)}) async-start(bf16[32,100,768]{2,1,0:T(8,128)(2,1)} %copy.9), calls=%async_computation | async-start | bytes 10223616 | tf_op jit(solution)/shard_map/all_to_all | solution.py:172
  32.5 0.0 copy-done
  32.5 0.1 dynamic_slice.3
  32.6 0.1 iota_subtract_fusion
  32.6 0.1 sub.72
  32.8 0.8 fusion.55.mask_ref
  33.6 1.0 fusion.47.order_ref
  34.6 1.3 fusion.15.e_ref
  36.0 59.6 %all-to-all-done.rx_ref = bf16[32,100,768]{2,1,0:T(8,128)(2,1)} async-done(((bf16[32,100,768]{2,1,0:T(8,128)(2,1)}), bf16[32,100,768]{2,1,0:T(8,128)(2,1)}, u32[]{:S(2)}, u32[]{:S(2)}) %all-to-all-start) | async-done | bytes 4915232 | tf_op jit(solution)/shard_map/all_to_all | solution.py:172
  95.6 0.6 broadcast_in_dim.8.first_ref
  96.2 30.3 %butterfly.1 = bf16[128,56,256]{2,1,0:T(8,128)(2,1)} custom-call(bf16[32,100,768]{2,1,0:T(8,128)(2,1)} %all-to-all-done.rx_ref, bf16[5,2,256,256]{3,2,1,0:T(8,128)(2,1)} %fusion.15.e_ref, f32[112,256]{1,0:T(8,128)} %fusion.55.mask_ref, s32[8,256]{1,0:T(8,128)} %broadcast_in_dim.8.first_ref, bf16[224,256]{1,0:T(8,128)(2,1)} %fusion.47.order_ref), custom_call_target="tpu_custom_call" | custom-call | tf_op jit(solution)/shard_map/butterfly/pallas_call | solution.py:108
  126.5 13.0 %all-to-all-start.1 = ((bf16[128,56,256]{2,1,0:T(8,128)(2,1)}), bf16[128,56,256]{2,1,0:T(8,128)(2,1)}, u32[]{:S(2)}, u32[]{:S(2)}) async-start(bf16[128,56,256]{2,1,0:T(8,128)(2,1)} %butterfly.1), calls=%async_computation.1 | async-start | bytes 7340032 | tf_op jit(solution)/shard_map/all_to_all | solution.py:178
  139.5 0.2 reshape.37
  139.7 0.2 reshape.38
  140.0 2.6 %fusion.26.order_ref = bf16[400,448]{1,0:T(8,128)(2,1)} fusion(s32[400]{0:T(512)S(1)} %get-tuple-element.25, s32[400]{0:T(512)S(1)} %get-tuple-element.35, s32[400]{0:T(512)S(1)} %get-tuple-element.26, s32[400]{0:T(512)S(1)} %get-tuple-element.30, s32[400]{0:T(512)S(1)} %get-tuple-element.27, s32[400]{0:T(512)S(1)} %get-tuple-element.36, ...), kind=kLoop, calls=%fused_computation.41 | loop fusion | flops 4659200 | bytes 372800 | tf_op jit(solution)/shard_map/convert_element_type | solution.py:56
  142.6 28.5 %multiply_convert_fusion.1 = (bf16[640,2560]{1,0:T(8,128)(2,1)S(1)}, bf16[640,2560]{1,0:T(8,128)(2,1)S(1)}) fusion(s32[640]{0:T(1024)S(1)} %reshape.38, f32[640]{0:T(1024)S(1)} %get-tuple-element.7, f32[640]{0:T(1024)S(1)} %get-tuple-element.8), kind=kLoop, calls=%fused_computation.7 | loop fusion | flops 21299200 | bytes 6561280 | tf_op jit(solution)/shard_map/convert
  171.1 3.1 %pad_maximum_fusion.table_ref = bf16[1280,2560]{1,0:T(8,128)(2,1)} fusion(bf16[640,2560]{1,0:T(8,128)(2,1)S(1)} %get-tuple-element.6, bf16[640,2560]{1,0:T(8,128)(2,1)S(1)} %get-tuple-element.5), kind=kLoop, calls=%fused_computation.5 | loop fusion | flops 13107200 | bytes 13107200 | tf_op jit(solution)/shard_map/concatenate | solution.py:162
  174.3 12.6 %all-to-all-done.1.u_ref = bf16[128,56,256]{2,1,0:T(8,128)(2,1)} async-done(((bf16[128,56,256]{2,1,0:T(8,128)(2,1)}), bf16[128,56,256]{2,1,0:T(8,128)(2,1)}, u32[]{:S(2)}, u32[]{:S(2)}) %all-to-all-start.1) | async-done | bytes 3670048 | tf_op jit(solution)/shard_map/all_to_all | solution.py:178
  186.9 17.0 %fourier.1 = bf16[5,256,2560]{2,1,0:T(8,128)(2,1)} custom-call(bf16[128,56,256]{2,1,0:T(8,128)(2,1)} %all-to-all-done.1.u_ref, bf16[400,448]{1,0:T(8,128)(2,1)} %fusion.26.order_ref, bf16[1280,2560]{1,0:T(8,128)(2,1)} %pad_maximum_fusion.table_ref), custom_call_target="tpu_custom_call" | custom-call | tf_op jit(solution)/shard_map/fourier/pallas_call | solution.py:139
  (19 shorter events, 0.2 us)
Async XLA Ops:
  23.7 8.8 %copy-start = (s32[640]{0:T(1024)S(1)}, s32[640]{0:T(1024)}, u32[]{:S(2)}) copy-start(s32[640]{0:T(1024)} %param.5) | copy-start | bytes 7684
  23.7 71.9 %all-to-all-start = ((bf16[32,100,768]{2,1,0:T(8,128)(2,1)}), bf16[32,100,768]{2,1,0:T(8,128)(2,1)}, u32[]{:S(2)}, u32[]{:S(2)}) async-start(bf16[32,100,768]{2,1,0:T(8,128)(2,1)} %copy.9), calls=%async_computation | async-start | bytes 10223616 | tf_op jit(solution)/shard_map/all_to_all | solution.py:172
  126.5 60.4 %all-to-all-start.1 = ((bf16[128,56,256]{2,1,0:T(8,128)(2,1)}), bf16[128,56,256]{2,1,0:T(8,128)(2,1)}, u32[]{:S(2)}, u32[]{:S(2)}) async-start(bf16[128,56,256]{2,1,0:T(8,128)(2,1)} %butterfly.1), calls=%async_computation.1 | async-start | bytes 7340032 | tf_op jit(solution)/shard_map/all_to_all | solution.py:178

commit v2 on v1

v2 whole, which is shorter than its diff:
```python
import math

import jax
import jax.numpy as jnp
import numpy as np
from jax import lax
from jax.experimental import pallas as pl
from jax.experimental.pallas import tpu as pltpu
from jax.sharding import PartitionSpec as P

NLON = 2560
SECTIONS = 5
BLOCKS = 32
BANDS = 4
DEG = 20
OWN = 5
CH = 512
HALF = 256
ROWS = DEG * OWN
PADR = 112
SLOT = 56
PAIR = 2 * PADR


def select_matrices():
    shape = (SECTIONS, 2, 256, PAIR)
    s, v, q, lane = (lax.broadcasted_iota(jnp.int32, shape, d) for d in range(4))
    part = (lane // PADR) ^ v
    inner = lane % PADR
    hit = (q == s * 40 + (inner % DEG) * 2 + part) & (inner < ROWS)
    return hit.astype(jnp.bfloat16)


def diagonal_mask():
    row = lax.broadcasted_iota(jnp.int32, (PADR, PAIR), 0)
    inner = lax.broadcasted_iota(jnp.int32, (PADR, PAIR), 1) % PADR
    hit = (row // DEG == inner // DEG) & (row < ROWS) & (inner < ROWS)
    return hit.astype(jnp.float32)


def send_order():
    row = lax.broadcasted_iota(jnp.int32, (BANDS * SLOT, PAIR), 0)
    col = lax.broadcasted_iota(jnp.int32, (BANDS * SLOT, PAIR), 1)
    band, inner = row // SLOT, row % SLOT
    part, kr = inner // 25, inner % 25
    want = part * PADR + (kr // 5) * DEG + 5 * band + kr % 5
    return ((col == want) & (inner < 50)).astype(jnp.bfloat16)


def fill_pack_order(order):
    shape = (4 * 104, DEG * 32)
    row = lax.broadcasted_iota(jnp.int32, shape, 0)
    col = lax.broadcasted_iota(jnp.int32, shape, 1)
    owner = (row >= 104).astype(jnp.int32) + (row >= 208).astype(jnp.int32) + (row >= 312).astype(jnp.int32)
    inner = row - 104 * owner
    k = sum((inner >= DEG * i).astype(jnp.int32) for i in range(1, OWN))
    base = (inner - DEG * k) * 32 + OWN * owner + k
    ahead = jnp.where(inner < ROWS, col - base, -1)
    for v in range(4):
        order[v] = (ahead == 4 * v).astype(jnp.float32).astype(jnp.bfloat16)


def pack_rows(src, order_ref, out_ref):
    for group in range(BLOCKS // 4):
        start = 4 * OWN * group
        at = start // 16 * 16
        window = src[:, at:at + 32, :]
        window = window.reshape(DEG * 32, window.shape[2])
        y = jnp.dot(order_ref[(start - at) // 4], window, preferred_element_type=jnp.float32)
        for d in range(4):
            out_ref[4 * group + d] = y[104 * d:104 * d + ROWS].astype(jnp.bfloat16)


def pack_factors_kernel(f_ref, eye_ref, out_ref, turned, order):
    fill_pack_order(order)
    for o in range(DEG):
        left = jnp.concatenate([f_ref[s, o].reshape(2 * DEG, OWN * BLOCKS) for s in range(SECTIONS)], axis=0)
        y = lax.dot_general(left, eye_ref[...], (((0,), (0,)), ((), ())), preferred_element_type=jnp.float32)
        turned[o] = y.astype(jnp.bfloat16)
    pack_rows(turned, order, out_ref)


def pack_factors(factors):
    return pl.pallas_call(
        pack_factors_kernel,
        out_shape=jax.ShapeDtypeStruct((BLOCKS, ROWS, 256), jnp.bfloat16),
        scratch_shapes=[pltpu.VMEM((DEG, OWN * BLOCKS, 256), jnp.bfloat16), pltpu.VMEM((4, 416, 640), jnp.bfloat16)],
        compiler_params=pltpu.CompilerParams(vmem_limit_bytes=60 << 20),
        name="pack_factors",
    )(factors.transpose(0, 2, 3, 1, 4), jnp.asarray(np.eye(200, 256), jnp.bfloat16))


def pack_coefficients_kernel(x_ref, out_ref, order):
    @pl.when(pl.program_id(0) == 0)
    def _():
        fill_pack_order(order)

    pack_rows(x_ref, order, out_ref)


def pack_coefficients(x):
    return pl.pallas_call(
        pack_coefficients_kernel,
        out_shape=jax.ShapeDtypeStruct((BLOCKS, ROWS, CH), jnp.bfloat16),
        grid=(2,),
        in_specs=[pl.BlockSpec((DEG, OWN * BLOCKS, HALF), lambda i: (0, 0, i))],
        out_specs=pl.BlockSpec((BLOCKS, ROWS, HALF), lambda i: (0, 0, i)),
        scratch_shapes=[pltpu.VMEM((4, 416, 640), jnp.bfloat16)],
        compiler_params=pltpu.CompilerParams(vmem_limit_bytes=60 << 20),
        name="pack_coefficients",
    )(x)


def receive_order():
    row = lax.broadcasted_iota(jnp.int32, (400, 8 * SLOT), 0)
    col = lax.broadcasted_iota(jnp.int32, (400, 8 * SLOT), 1)
    part, lat = row // 200, (row // 40) % 5
    src, k = (row % 40) // 5, row % 5
    return (col == src * SLOT + part * 25 + k * 5 + lat).astype(jnp.bfloat16)


def lower_block(s, group, j):
    if s < 3:
        return 8 * group + (j >> s) * (2 << s) + (j & ((1 << s) - 1))
    step = 16 if s == 3 else 8
    return 2 * group + j // 2 + step * (j % 2)


def section_kernel(rf_ref, e_ref, mask_ref, first_ref, near_ref, far_ref, fc):
    zeros_f = jnp.zeros((16, 256), jnp.bfloat16)

    def load(b, carry):
        fc[b, pl.ds(96, 16), :] = zeros_f
        fc[b, pl.ds(0, ROWS), :] = rf_ref[b]
        return carry

    lax.fori_loop(0, BLOCKS, load, 0)
    lane_high = lax.broadcasted_iota(jnp.int32, (8, PAIR), 1) // PADR
    mask = mask_ref[...]
    for s in range(SECTIONS):
        lows = [(g, j, lower_block(s, g, j)) for g in range(4) for j in range(4)]
        for v in range(2):
            left = jnp.concatenate([fc[low + (v << s)] for _, _, low in lows], axis=0)
            f = jnp.dot(left, e_ref[s, v], preferred_element_type=jnp.float32)
            for i, (g, j, low) in enumerate(lows):
                keep = mask
                if s == 0:
                    start = DEG * (low + lane_high)
                    live = (start >= first_ref[...]).astype(jnp.float32)
                    keep = mask * live[0:1, :]
                piece = (f[i * PADR:(i + 1) * PADR] * keep).astype(jnp.bfloat16)
                if s < 3:
                    near_ref[g, 4 * s + j, pl.ds(v * PADR, PADR), :] = piece
                else:
                    far_ref[g, 4 * (s - 3) + j, pl.ds(v * PADR, PADR), :] = piece


def section_factors(rf, first):
    return pl.pallas_call(
        section_kernel,
        out_shape=[
            jax.ShapeDtypeStruct((4, 12, PAIR, PAIR), jnp.bfloat16),
            jax.ShapeDtypeStruct((4, 8, PAIR, PAIR), jnp.bfloat16),
        ],
        scratch_shapes=[pltpu.VMEM((BLOCKS, PADR, 256), jnp.bfloat16)],
        compiler_params=pltpu.CompilerParams(vmem_limit_bytes=58 << 20),
        name="section_factors",
    )(rf, select_matrices(), diagonal_mask(), first)


def butterfly_kernel(rx_ref, near_ref, far_ref, order_ref, out_ref, xa, xb, xc, xd):
    step = pl.program_id(0)

    @pl.when(step == 0)
    def _():
        for b in range(8):
            xa[b, pl.ds(96, 16), :] = jnp.zeros((16, CH), jnp.bfloat16)

    @pl.when(step < 4)
    def _():
        for b in range(8):
            xa[b, pl.ds(0, ROWS), :] = rx_ref[b]
        src, dst = xa, xb
        for s in range(3):
            base = 8 * step if s == 2 else 0
            out = xc if s == 2 else dst
            for j in range(4):
                low = lower_block(s, 0, j)
                high = low + (1 << s)
                right = jnp.concatenate([src[low], src[high]], axis=0)
                y = jnp.dot(near_ref[0, 4 * s + j], right, preferred_element_type=jnp.float32).astype(jnp.bfloat16)
                out[base + low] = y[:PADR]
                out[base + high] = y[PADR:]
            src, dst = dst, src

    @pl.when(step >= 4)
    def _():
        first = 2 * (step - 4)
        for j in range(4):
            r, h = j // 2, j % 2
            low = first + r + 16 * h
            right = jnp.concatenate([xc[low], xc[low + 8]], axis=0)
            y = jnp.dot(far_ref[0, j], right, preferred_element_type=jnp.float32).astype(jnp.bfloat16)
            xd[r, 2 * h] = y[:PADR]
            xd[r, 2 * h + 1] = y[PADR:]
        for j in range(4):
            r, h = j // 2, j % 2
            right = jnp.concatenate([xd[r, h], xd[r, h + 2]], axis=0)
            y = jnp.dot(far_ref[0, 4 + j], right, preferred_element_type=jnp.float32).astype(jnp.bfloat16)
            for half in range(2):
                rows = y[half * PADR:(half + 1) * PADR]
                right = jnp.concatenate([rows[:, :HALF], rows[:, HALF:]], axis=0)
                z = jnp.dot(order_ref[...], right, preferred_element_type=jnp.float32)
                for band in range(BANDS):
                    out_ref[h + 2 * half, r, band] = z[band * SLOT:(band + 1) * SLOT].astype(jnp.bfloat16)


def butterfly(rx, near, far):
    early = lambda i: jnp.minimum(i, 3)
    late = lambda i: jnp.maximum(i - 4, 0)
    rows = pl.pallas_call(
        butterfly_kernel,
        out_shape=jax.ShapeDtypeStruct((4, 8, BANDS, SLOT, HALF), jnp.bfloat16),
        grid=(8,),
        in_specs=[
            pl.BlockSpec((8, ROWS, CH), lambda i: (early(i), 0, 0)),
            pl.BlockSpec((1, 12, PAIR, PAIR), lambda i: (early(i), 0, 0, 0)),
            pl.BlockSpec((1, 8, PAIR, PAIR), lambda i: (late(i), 0, 0, 0)),
            pl.BlockSpec((BANDS * SLOT, PAIR), lambda i: (0, 0)),
        ],
        out_specs=pl.BlockSpec((4, 2, BANDS, SLOT, HALF), lambda i: (0, late(i), 0, 0, 0)),
        scratch_shapes=[
            pltpu.VMEM((8, PADR, CH), jnp.bfloat16),
            pltpu.VMEM((8, PADR, CH), jnp.bfloat16),
            pltpu.VMEM((BLOCKS, PADR, CH), jnp.bfloat16),
            pltpu.VMEM((2, 4, PADR, CH), jnp.bfloat16),
        ],
        compiler_params=pltpu.CompilerParams(vmem_limit_bytes=56 << 20),
        name="butterfly",
    )(rx, near, far, send_order())
    return rows.reshape(BLOCKS * BANDS, SLOT, HALF)


def mirror_order():
    row = lax.broadcasted_iota(jnp.int32, (256, 256), 0)
    lane = lax.broadcasted_iota(jnp.int32, (256, 256), 1)
    return (row + lane == 256).astype(jnp.bfloat16)


def fourier_kernel(u_ref, order_ref, mirror_ref, table_ref, middle_ref, out_ref, v, vt, edge, buf, sem):
    step = pl.program_id(0)
    slot = step % 2
    tile = 256

    def copies(at, into):
        near = pltpu.make_async_copy(buf.at[into, 0], out_ref.at[:, :, pl.ds((4 - at) * tile, tile)], sem.at[into, 0])
        far = pltpu.make_async_copy(buf.at[into, 1], out_ref.at[:, :, pl.ds((5 + at) * tile, tile)], sem.at[into, 1])
        return near, far

    def sums(table):
        even = jnp.dot(vt[:, :640], table[:640], preferred_element_type=jnp.float32)
        odd = jnp.dot(vt[:, 640:], table[640:], preferred_element_type=jnp.float32)
        return even, odd

    @pl.when(step == 0)
    def _():
        for g in range(16):
            piece = u_ref[pl.ds(8 * g, 8)].reshape(8 * SLOT, HALF)
            y = jnp.dot(order_ref[...], piece, preferred_element_type=jnp.float32)
            for p in range(2):
                for r in range(5):
                    at = p * 200 + r * 40
                    v[r, pl.ds(p * 640 + 40 * g, 40), :] = y[at:at + 40].astype(jnp.bfloat16)
        for r in range(5):
            vt[pl.ds(r * HALF, HALF), :] = v[r].T
        even, odd = sums(middle_ref[...])
        edge[...] = even - odd

    @pl.when(step >= 2)
    def _():
        for copy in copies(step - 2, slot):
            copy.wait()

    even, odd = sums(table_ref[...])
    near = (even + odd).astype(jnp.bfloat16)
    far = (even - odd).astype(jnp.bfloat16)
    turned = jnp.dot(far, mirror_ref[...], preferred_element_type=jnp.float32)
    lane = lax.broadcasted_iota(jnp.int32, (5 * HALF, 128), 1)
    head = jnp.where(lane == 0, edge[...], turned[:, :128]).astype(jnp.bfloat16)
    tail = turned[:, 128:].astype(jnp.bfloat16)
    edge[...] = far[:, :128].astype(jnp.float32)
    for r in range(5):
        rows = slice(r * HALF, (r + 1) * HALF)
        buf[slot, 0, r] = near[rows]
        buf[slot, 1, r, :, pl.ds(0, 128)] = head[rows]
        buf[slot, 1, r, :, pl.ds(128, 128)] = tail[rows]
    for copy in copies(step, slot):
        copy.start()

    @pl.when(step == 4)
    def _():
        for copy in copies(3, 1) + copies(4, 0):
            copy.wait()


def fourier(u, table):
    return pl.pallas_call(
        fourier_kernel,
        out_shape=jax.ShapeDtypeStruct((5, HALF, NLON), jnp.bfloat16),
        grid=(5,),
        in_specs=[
            pl.BlockSpec((BLOCKS * BANDS, SLOT, HALF), lambda j: (0, 0, 0)),
            pl.BlockSpec((400, 8 * SLOT), lambda j: (0, 0)),
            pl.BlockSpec((256, 256), lambda j: (0, 0)),
            pl.BlockSpec((1280, 256), lambda j: (0, 4 - j)),
            pl.BlockSpec((1280, 128), lambda j: (0, 10)),
        ],
        out_specs=pl.BlockSpec(memory_space=pl.ANY),
        scratch_shapes=[
            pltpu.VMEM((5, 1280, HALF), jnp.bfloat16),
            pltpu.VMEM((5 * HALF, 1280), jnp.bfloat16),
            pltpu.VMEM((5 * HALF, 128), jnp.float32),
            pltpu.VMEM((2, 2, 5, HALF, 256), jnp.bfloat16),
            pltpu.SemaphoreType.DMA((2, 2)),
        ],
        compiler_params=pltpu.CompilerParams(vmem_limit_bytes=60 << 20),
        name="fourier",
    )(u, receive_order(), mirror_order(), table, table)


def fourier_table(ids):
    longitude = jnp.arange(NLON // 2 + 128, dtype=jnp.int32)
    phases = ids[:, None] * longitude[None, :] % NLON
    angles = phases.astype(jnp.float32) * (2.0 * math.pi / NLON)
    weight = jnp.where(ids == 0, 1.0, 2.0).astype(jnp.float32) / math.sqrt(2.0 * ids.shape[0])
    cosine_part = weight[:, None] * jnp.cos(angles)
    sine_part = -weight[:, None] * jnp.sin(angles)
    return jnp.concatenate([cosine_part, sine_part], axis=0).astype(jnp.bfloat16)


def body(coefficients, factors, wave_ids):
    wave_pos = lax.axis_index("wave")
    lev_pos = lax.axis_index("lev")
    rf = lax.all_to_all(pack_factors(factors), "wave", 0, 0, tiled=True)
    send_x, rf = lax.optimization_barrier((pack_coefficients(coefficients), rf))
    rx = lax.all_to_all(send_x, "wave", 0, 0, tiled=True)
    own_ids = lax.dynamic_slice_in_dim(wave_ids, lev_pos * (OWN * BLOCKS) + wave_pos * OWN, OWN, 0)
    first = (own_ids[:, None] - jnp.arange(DEG, dtype=jnp.int32)[None, :]).reshape(ROWS)
    first = jnp.pad(first, (0, PADR - ROWS))
    first = jnp.broadcast_to(jnp.concatenate([first, first])[None, :], (8, PAIR))
    near, far = section_factors(rf, first)
    rows = butterfly(rx, near, far)
    u = lax.all_to_all(rows, ("wave", "lev"), 0, 0, tiled=True)
    ids = wave_ids.reshape(BANDS, BLOCKS, OWN).transpose(1, 0, 2).reshape(-1)
    return fourier(u, fourier_table(ids))


def solution(mesh):
    in_specs = (P("wave", "lev", None), P(None, None, "wave", None, "lev"), P())
    out_specs = P(("wave", "lev"), None, None)
    return jax.shard_map(body, mesh=mesh, in_specs=in_specs, out_specs=out_specs, check_vma=False)
```

time: 204 us -> 174 us (0.85)
  local copies, waits for them, and re-layouts: 21.8 us -> 4.33 us
  other arithmetic: 40.5 us -> 25.3 us
  waiting for transfers between devices: 72.2 us -> 74.3 us
    all_to_all x1, waiting for transfers between devices: 12.6 us -> 24.9 us  [body(): u = lax.all_to_all(rows, ('wave', 'lev'), 0, 0, tiled=True)]
    another operation x1, other arithmetic: 28.5 us -> 16.5 us
    all_to_all x1 -> x2, waiting for transfers between devices: 59.6 us -> 49.4 us  [the longest x1 31.4 us: body(): rx = lax.all_to_all(send_x, 'wave', 0, 0, tiled=True)]
    reshape x2 -> x0, local copies, waits for them, and re-layouts: 9.52 us -> none  [the longest x1 5.1 us: body(): joined.reshape(DEG, BLOCKS, OWN, 768).transpose(1, 2, 0, 3)]
    transpose x2 -> x0, local copies, waits for them, and re-layouts: 5.45 us -> none  [the longest x1 4.28 us: body(): flat = factors.transpose(2, 4, 0, 3, 1).reshape(DEG, OWN * BLOCKS, 200)]
    all_to_all x1 -> x2, starting transfers between devices: 8.78 us -> 13 us  [the longest x1 8.58 us: body(): rf = lax.all_to_all(pack_factors(factors), 'wave', 0, 0, tiled=True)]
    all_to_all x1, starting transfers between devices: 13 us -> 9.43 us  [body(): u = lax.all_to_all(rows, ('wave', 'lev'), 0, 0, tiled=True)]
    pallas_call x1, Pallas kernels: 17 us -> 14 us  [fourier(): pl.pallas_call(fourier_kernel, out_shape=jax.ShapeDtypeStruct((5, HALF, N...]
  transfers between devices with their start and end apart: 2 -> 3, of which waited for: 2 -> 3; matrix products, arithmetic and copies ran while one was open for 19% -> 15% of each run, Pallas kernels for 0% -> 8%
where the time goes in v2:
time: 174 us; the launch traced here: 173 us
  waiting for transfers between devices  74.3 us (43%)
  Pallas kernels  46.2 us (27%)
  other arithmetic  25.3 us (15%)
  starting transfers between devices  22.5 us (13%)
  local copies, waits for them, and re-layouts  4.33 us (2%)
    all_to_all x1, waiting for transfers between devices, body(): rx = lax.all_to_all(send_x, 'wave', 0, 0, tiled=True)  31.4 us
    all_to_all x1, waiting for transfers between devices, body(): u = lax.all_to_all(rows, ('wave', 'lev'), 0, 0, tiled=True)  24.9 us
    all_to_all x1, waiting for transfers between devices, body(): rf = lax.all_to_all(pack_factors(factors), 'wave', 0, 0, tiled=True)  18 us
    another operation x1, other arithmetic  16.5 us
    pallas_call x1, Pallas kernels, fourier(): pl.pallas_call(fourier_kernel, out_shape=jax.ShapeDtypeStruct((5, HALF, N...  14 us
    pallas_call x1, Pallas kernels, butterfly(): pl.pallas_call(butterfly_kernel, out_shape=jax.ShapeDtypeStruct((4, 8, BA...  13.6 us
    all_to_all x1, starting transfers between devices, body(): u = lax.all_to_all(rows, ('wave', 'lev'), 0, 0, tiled=True)  9.43 us
    all_to_all x1, starting transfers between devices, body(): rf = lax.all_to_all(pack_factors(factors), 'wave', 0, 0, tiled=True)  8.58 us
  transfers between devices with their start and end apart: 3, of which 3 were waited for; matrix products, arithmetic and copies ran while one was open for 15% of the time, Pallas kernels for 8%

profile of v2, /device:TPU:1, one launch (start us, length us, event | category | flops | bytes accessed | tf_op | source)
XLA Modules:
  0.0 172.9 jit_solution(12360402908365341499)
XLA Ops:
  0.0 5.2 %pack_factors.1 = bf16[32,100,256]{2,1,0:T(8,128)(2,1)} custom-call(bf16[5,20,20,2,160]{4,3,2,1,0:T(2,128)(2,1)} %bitcast.4, bf16[200,256]{1,0:T(8,128)(2,1)} %constant.169.clone.eye_ref), custom_call_target="tpu_custom_call" | custom-call | tf_op jit(solution)/shard_map/pack_factors/pallas_call | solution.py:84
  5.2 8.6 %all-to-all-start = ((bf16[32,100,256]{2,1,0:T(8,128)(2,1)}), bf16[32,100,256]{2,1,0:T(8,128)(2,1)S(1)}, u32[]{:S(2)}, u32[]{:S(2)}) async-start(bf16[32,100,256]{2,1,0:T(8,128)(2,1)} %pack_factors.1), calls=%async_computation | async-start | bytes 3407872 | tf_op jit(solution)/shard_map/all_to_all | solution.py:344
  13.8 6.1 %pack_coefficients.1 = bf16[32,100,512]{2,1,0:T(8,128)(2,1)} custom-call(bf16[20,160,512]{2,1,0:T(8,128)(2,1)} %x_ref.1), custom_call_target="tpu_custom_call" | custom-call | tf_op jit(solution)/shard_map/pack_coefficients/pallas_call | solution.py:102
  19.9 0.0 copy-start.2
  19.9 18.0 %all-to-all-done.rf_ref = bf16[32,100,256]{2,1,0:T(8,128)(2,1)S(1)} async-done(((bf16[32,100,256]{2,1,0:T(8,128)(2,1)}), bf16[32,100,256]{2,1,0:T(8,128)(2,1)S(1)}, u32[]{:S(2)}, u32[]{:S(2)}) %all-to-all-start) | async-done | bytes 1638432 | tf_op jit(solution)/shard_map/all_to_all | solution.py:344
  37.9 0.0 copy-start.1
  37.9 1.3 copy-done.1
  39.2 4.5 %all-to-all-start.1 = ((bf16[32,100,512]{2,1,0:T(8,128)(2,1)}), bf16[32,100,512]{2,1,0:T(8,128)(2,1)S(1)}, u32[]{:S(2)}, u32[]{:S(2)}) async-start(bf16[32,100,512]{2,1,0:T(8,128)(2,1)} %pack_coefficients.1), calls=%async_computation.1 | async-start | bytes 6815744 | tf_op jit(solution)/shard_map/all_to_all | solution.py:346
  43.6 0.0 copy-done.2
  43.6 0.1 dynamic_slice.3
  43.7 0.1 iota_subtract_fusion
  43.8 0.1 sub.72
  43.9 0.1 pad_add_fusion
  44.1 0.8 fusion.54.mask_ref
  44.9 1.0 fusion.46.order_ref
  45.9 1.3 fusion.13.e_ref
  47.2 0.6 broadcast_in_dim.8.first_ref
  47.8 7.2 %section_factors.1 = (bf16[4,12,224,224]{3,2,1,0:T(8,128)(2,1)}, bf16[4,8,224,224]{3,2,1,0:T(8,128)(2,1)}) custom-call(bf16[32,100,256]{2,1,0:T(8,128)(2,1)} %copy-done.1, bf16[5,2,256,224]{3,2,1,0:T(8,128)(2,1)} %fusion.13.e_ref, f32[112,224]{1,0:T(8,128)} %fusion.54.mask_ref, s32[8,224]{1,0:T(8,128)} %broadcast_in_dim.8.first_ref), custom_call_target="tpu_custom_call" | custom-call | tf_op jit(solution)/shard_map/section_factors/pallas_call | solution.py:159
  55.0 31.4 %all-to-all-done.1.rx_ref = bf16[32,100,512]{2,1,0:T(8,128)(2,1)S(1)} async-done(((bf16[32,100,512]{2,1,0:T(8,128)(2,1)}), bf16[32,100,512]{2,1,0:T(8,128)(2,1)S(1)}, u32[]{:S(2)}, u32[]{:S(2)}) %all-to-all-start.1) | async-done | bytes 3276832 | tf_op jit(solution)/shard_map/all_to_all | solution.py:346
  86.4 0.0 copy-start
  86.4 1.8 %copy-done = bf16[32,100,512]{2,1,0:T(8,128)(2,1)} copy-done((bf16[32,100,512]{2,1,0:T(8,128)(2,1)}, bf16[32,100,512]{2,1,0:T(8,128)(2,1)S(1)}, u32[]{:S(2)}) %copy-start) | copy-done | bytes 3276824
  88.3 13.6 %butterfly.1 = bf16[4,8,4,56,256]{4,3,2,1,0:T(8,128)(2,1)} custom-call(bf16[32,100,512]{2,1,0:T(8,128)(2,1)} %copy-done, bf16[4,12,224,224]{3,2,1,0:T(8,128)(2,1)} %get-tuple-element.11.near_ref, bf16[4,8,224,224]{3,2,1,0:T(8,128)(2,1)} %get-tuple-element.12.far_ref, bf16[224,224]{1,0:T(8,128)(2,1)} %fusion.46.order_ref), custom_call_target="tpu_custom_call" | custom-call | tf_op jit(solution)/shard_map/butterfly/pallas_call | solution.py:221
  101.9 9.4 %all-to-all-start.2 = ((bf16[128,56,256]{2,1,0:T(8,128)(2,1)}), bf16[128,56,256]{2,1,0:T(8,128)(2,1)}, u32[]{:S(2)}, u32[]{:S(2)}) async-start(bf16[128,56,256]{2,1,0:T(8,128)(2,1)} %bitcast.3), calls=%async_computation.2 | async-start | bytes 7340032 | tf_op jit(solution)/shard_map/all_to_all | solution.py:353
  111.3 0.2 reshape.29
  111.6 0.2 reshape.30
  111.9 0.7 fusion.30.mirror_ref
  112.6 2.5 %fusion.24.order_ref = bf16[400,448]{1,0:T(8,128)(2,1)} fusion(s32[400]{0:T(512)S(1)} %get-tuple-element.33, s32[400]{0:T(512)S(1)} %get-tuple-element.43, s32[400]{0:T(512)S(1)} %get-tuple-element.34, s32[400]{0:T(512)S(1)} %get-tuple-element.38, s32[400]{0:T(512)S(1)} %get-tuple-element.35, s32[400]{0:T(512)S(1)} %get-tuple-element.44, ...), kind=kLoop, calls=%fused_computation.38 | loop fusion | flops 4659200 | bytes 372800 | tf_op jit(solution)/shard_map/convert_element_type | solution.py:119
  115.1 16.5 %multiply_convert_fusion.1 = (bf16[640,1408]{1,0:T(8,128)(2,1)S(1)}, bf16[640,1408]{1,0:T(8,128)(2,1)S(1)}) fusion(s32[640]{0:T(1024)S(1)} %reshape.30, f32[640]{0:T(1024)S(1)} %get-tuple-element.15, f32[640]{0:T(1024)S(1)} %get-tuple-element.16), kind=kLoop, calls=%fused_computation.10 | loop fusion | flops 11714560 | bytes 3612160 | tf_op jit(solution)/shard_map/convert
  131.6 2.2 %pad_maximum_fusion.table_ref.middle_ref = bf16[1280,1408]{1,0:T(8,128)(2,1)} fusion(bf16[640,1408]{1,0:T(8,128)(2,1)S(1)} %get-tuple-element.14, bf16[640,1408]{1,0:T(8,128)(2,1)S(1)} %get-tuple-element.13), kind=kLoop, calls=%fused_computation.8 | loop fusion | flops 7208960 | bytes 7208960 | tf_op jit(solution)/shard_map/concatenate | solution.py:338
  133.8 24.9 %all-to-all-done.2.u_ref = bf16[128,56,256]{2,1,0:T(8,128)(2,1)} async-done(((bf16[128,56,256]{2,1,0:T(8,128)(2,1)}), bf16[128,56,256]{2,1,0:T(8,128)(2,1)}, u32[]{:S(2)}, u32[]{:S(2)}) %all-to-all-start.2) | async-done | bytes 3670048 | tf_op jit(solution)/shard_map/all_to_all | solution.py:353
  158.7 14.0 %fourier.1 = bf16[5,256,2560]{2,1,0:T(8,128)(2,1)} custom-call(bf16[128,56,256]{2,1,0:T(8,128)(2,1)} %all-to-all-done.2.u_ref, bf16[400,448]{1,0:T(8,128)(2,1)} %fusion.24.order_ref, bf16[256,256]{1,0:T(8,128)(2,1)} %fusion.30.mirror_ref, bf16[1280,1408]{1,0:T(8,128)(2,1)} %pad_maximum_fusion.table_ref.middle_ref, ...), custom_call_target="tpu_custom_call" | custom-call | tf_op jit(solution)/shard_map/fourier/pallas_call | solution.py:307
  (18 shorter events, 0.2 us)
Async XLA Ops:
  5.2 32.7 %all-to-all-start = ((bf16[32,100,256]{2,1,0:T(8,128)(2,1)}), bf16[32,100,256]{2,1,0:T(8,128)(2,1)S(1)}, u32[]{:S(2)}, u32[]{:S(2)}) async-start(bf16[32,100,256]{2,1,0:T(8,128)(2,1)} %pack_factors.1), calls=%async_computation | async-start | bytes 3407872 | tf_op jit(solution)/shard_map/all_to_all | solution.py:344
  19.9 23.7 %copy-start.2 = (s32[640]{0:T(1024)S(1)}, s32[640]{0:T(1024)}, u32[]{:S(2)}) copy-start(s32[640]{0:T(1024)} %param.6) | copy-start | bytes 7684
  37.9 1.3 copy-start.1
  39.2 47.2 %all-to-all-start.1 = ((bf16[32,100,512]{2,1,0:T(8,128)(2,1)}), bf16[32,100,512]{2,1,0:T(8,128)(2,1)S(1)}, u32[]{:S(2)}, u32[]{:S(2)}) async-start(bf16[32,100,512]{2,1,0:T(8,128)(2,1)} %pack_coefficients.1), calls=%async_computation.1 | async-start | bytes 6815744 | tf_op jit(solution)/shard_map/all_to_all | solution.py:346
  86.4 1.9 %copy-start = (bf16[32,100,512]{2,1,0:T(8,128)(2,1)}, bf16[32,100,512]{2,1,0:T(8,128)(2,1)S(1)}, u32[]{:S(2)}) copy-start(bf16[32,100,512]{2,1,0:T(8,128)(2,1)S(1)} %all-to-all-done.1.rx_ref) | copy-start | bytes 9830404
  101.9 56.8 %all-to-all-start.2 = ((bf16[128,56,256]{2,1,0:T(8,128)(2,1)}), bf16[128,56,256]{2,1,0:T(8,128)(2,1)}, u32[]{:S(2)}, u32[]{:S(2)}) async-start(bf16[128,56,256]{2,1,0:T(8,128)(2,1)} %bitcast.3), calls=%async_computation.2 | async-start | bytes 7340032 | tf_op jit(solution)/shard_map/all_to_all | solution.py:353

commit v3 on v2

--- a/solution.py
+++ b/solution.py
@@ -15,7 +15,8 @@
 DEG = 20
 OWN = 5
 CH = 512
-HALF = 256
+PART = 256
+HALF = 128
 ROWS = DEG * OWN
 PADR = 112
 SLOT = 56
@@ -60,55 +61,81 @@
         order[v] = (ahead == 4 * v).astype(jnp.float32).astype(jnp.bfloat16)
 
 
-def pack_rows(src, order_ref, out_ref):
+def pack_rows(srcs, order, out_ref):
     for group in range(BLOCKS // 4):
         start = 4 * OWN * group
         at = start // 16 * 16
-        window = src[:, at:at + 32, :]
-        window = window.reshape(DEG * 32, window.shape[2])
-        y = jnp.dot(order_ref[(start - at) // 4], window, preferred_element_type=jnp.float32)
+        window = jnp.concatenate([src[:, at:at + 32, :].reshape(DEG * 32, src.shape[2]) for src in srcs], axis=1)
+        y = jnp.dot(order[(start - at) // 4], window, preferred_element_type=jnp.float32)
         for d in range(4):
             out_ref[4 * group + d] = y[104 * d:104 * d + ROWS].astype(jnp.bfloat16)
 
 
-def pack_factors_kernel(f_ref, eye_ref, out_ref, turned, order):
+def pack_first_kernel(f_ref, eye_ref, x_ref, out_ref, turned, order, xs, sem):
+    fetch = [
+        pltpu.make_async_copy(x_ref.at[:, :, pl.ds(p * PART, HALF)], xs.at[:, :, pl.ds(p * HALF, HALF)], sem.at[p])
+        for p in range(2)
+    ]
+
+    @pl.when(pl.program_id(0) == 0)
+    def _():
+        for copy in fetch:
+            copy.start()
+        fill_pack_order(order)
+        for o in range(DEG):
+            left = jnp.concatenate([f_ref[s, o].reshape(2 * DEG, OWN * BLOCKS) for s in range(SECTIONS)], axis=0)
+            y = lax.dot_general(left, eye_ref[...], (((0,), (0,)), ((), ())), preferred_element_type=jnp.float32)
+            turned[o] = y.astype(jnp.bfloat16)
+        pack_rows([turned], order, out_ref)
+
+    @pl.when(pl.program_id(0) == 1)
+    def _():
+        for copy in fetch:
+            copy.wait()
+        pack_rows([xs], order, out_ref)
+
+
+def pack_first(factors, x):
+    return pl.pallas_call(
+        pack_first_kernel,
+        out_shape=jax.ShapeDtypeStruct((BLOCKS, ROWS, 2 * PART), jnp.bfloat16),
+        grid=(2,),
+        in_specs=[
+            pl.BlockSpec((SECTIONS, DEG, DEG, 2, OWN * BLOCKS), lambda i: (0, 0, 0, 0, 0)),
+            pl.BlockSpec((200, 256), lambda i: (0, 0)),
+            pl.BlockSpec(memory_space=pl.ANY),
+        ],
+        out_specs=pl.BlockSpec((BLOCKS, ROWS, PART), lambda i: (0, 0, i)),
+        scratch_shapes=[
+            pltpu.VMEM((DEG, OWN * BLOCKS, 256), jnp.bfloat16),
+            pltpu.VMEM((4, 416, 640), jnp.bfloat16),
+            pltpu.VMEM((DEG, OWN * BLOCKS, PART), jnp.bfloat16),
+            pltpu.SemaphoreType.DMA((2,)),
+        ],
+        compiler_params=pltpu.CompilerParams(vmem_limit_bytes=60 << 20),
+        name="pack_first",
+    )(factors.transpose(0, 2, 3, 1, 4), jnp.asarray(np.eye(200, 256), jnp.bfloat16), x)
+
+
+def pack_second_kernel(re_ref, im_ref, out_ref, order):
     fill_pack_order(order)
-    for o in range(DEG):
-        left = jnp.concatenate([f_ref[s, o].reshape(2 * DEG, OWN * BLOCKS) for s in range(SECTIONS)], axis=0)
-        y = lax.dot_general(left, eye_ref[...], (((0,), (0,)), ((), ())), preferred_element_type=jnp.float32)
-        turned[o] = y.astype(jnp.bfloat16)
-    pack_rows(turned, order, out_ref)
-
-
-def pack_factors(factors):
+    pack_rows([re_ref, im_ref], order, out_ref)
+
+
+def pack_second(x):
     return pl.pallas_call(
-        pack_factors_kernel,
-        out_shape=jax.ShapeDtypeStruct((BLOCKS, ROWS, 256), jnp.bfloat16),
-        scratch_shapes=[pltpu.VMEM((DEG, OWN * BLOCKS, 256), jnp.bfloat16), pltpu.VMEM((4, 416, 640), jnp.bfloat16)],
-        compiler_params=pltpu.CompilerParams(vmem_limit_bytes=60 << 20),
-        name="pack_factors",
-    )(factors.transpose(0, 2, 3, 1, 4), jnp.asarray(np.eye(200, 256), jnp.bfloat16))
-
-
-def pack_coefficients_kernel(x_ref, out_ref, order):
-    @pl.when(pl.program_id(0) == 0)
-    def _():
-        fill_pack_order(order)
-
-    pack_rows(x_ref, order, out_ref)
-
-
-def pack_coefficients(x):
-    return pl.pallas_call(
-        pack_coefficients_kernel,
-        out_shape=jax.ShapeDtypeStruct((BLOCKS, ROWS, CH), jnp.bfloat16),
-        grid=(2,),
-        in_specs=[pl.BlockSpec((DEG, OWN * BLOCKS, HALF), lambda i: (0, 0, i))],
-        out_specs=pl.BlockSpec((BLOCKS, ROWS, HALF), lambda i: (0, 0, i)),
+        pack_second_kernel,
+        out_shape=jax.ShapeDtypeStruct((BLOCKS, ROWS, PART), jnp.bfloat16),
+        grid=(1,),
+        in_specs=[
+            pl.BlockSpec((DEG, OWN * BLOCKS, HALF), lambda i: (0, 0, 1)),
+            pl.BlockSpec((DEG, OWN * BLOCKS, HALF), lambda i: (0, 0, 3)),
+        ],
+        out_specs=pl.BlockSpec((BLOCKS, ROWS, PART), lambda i: (0, 0, 0)),
         scratch_shapes=[pltpu.VMEM((4, 416, 640), jnp.bfloat16)],
         compiler_params=pltpu.CompilerParams(vmem_limit_bytes=60 << 20),
-        name="pack_coefficients",
-    )(x)
+        name="pack_second",
+    )(x, x)
 
 
 def receive_order():
@@ -162,6 +189,17 @@
             jax.ShapeDtypeStruct((4, 12, PAIR, PAIR), jnp.bfloat16),
             jax.ShapeDtypeStruct((4, 8, PAIR, PAIR), jnp.bfloat16),
         ],
+        grid=(1,),
+        in_specs=[
+            pl.BlockSpec((BLOCKS, ROWS, 256), lambda i: (0, 0, 0)),
+            pl.BlockSpec((SECTIONS, 2, 256, PAIR), lambda i: (0, 0, 0, 0)),
+            pl.BlockSpec((PADR, PAIR), lambda i: (0, 0)),
+            pl.BlockSpec((8, PAIR), lambda i: (0, 0)),
+        ],
+        out_specs=[
+            pl.BlockSpec((4, 12, PAIR, PAIR), lambda i: (0, 0, 0, 0)),
+            pl.BlockSpec((4, 8, PAIR, PAIR), lambda i: (0, 0, 0, 0)),
+        ],
         scratch_shapes=[pltpu.VMEM((BLOCKS, PADR, 256), jnp.bfloat16)],
         compiler_params=pltpu.CompilerParams(vmem_limit_bytes=58 << 20),
         name="section_factors",
@@ -174,7 +212,7 @@
     @pl.when(step == 0)
     def _():
         for b in range(8):
-            xa[b, pl.ds(96, 16), :] = jnp.zeros((16, CH), jnp.bfloat16)
+            xa[b, pl.ds(96, 16), :] = jnp.zeros((16, PART), jnp.bfloat16)
 
     @pl.when(step < 4)
     def _():
@@ -207,38 +245,44 @@
             r, h = j // 2, j % 2
             right = jnp.concatenate([xd[r, h], xd[r, h + 2]], axis=0)
             y = jnp.dot(far_ref[0, 4 + j], right, preferred_element_type=jnp.float32).astype(jnp.bfloat16)
+            re = jnp.concatenate([y[:PADR, :HALF], y[PADR:, :HALF]], axis=1)
+            im = jnp.concatenate([y[:PADR, HALF:], y[PADR:, HALF:]], axis=1)
+            z = jnp.dot(order_ref[...], jnp.concatenate([re, im], axis=0), preferred_element_type=jnp.float32)
             for half in range(2):
-                rows = y[half * PADR:(half + 1) * PADR]
-                right = jnp.concatenate([rows[:, :HALF], rows[:, HALF:]], axis=0)
-                z = jnp.dot(order_ref[...], right, preferred_element_type=jnp.float32)
                 for band in range(BANDS):
-                    out_ref[h + 2 * half, r, band] = z[band * SLOT:(band + 1) * SLOT].astype(jnp.bfloat16)
-
-
-def butterfly(rx, near, far):
+                    piece = z[band * SLOT:(band + 1) * SLOT, half * HALF:(half + 1) * HALF]
+                    out_ref[h + 2 * half, r, band] = piece.astype(jnp.bfloat16)
+
+
+def butterfly_more_kernel(rx_ref, near_ref, far_ref, order_ref, rows_ref, out_ref, *scratch):
+    butterfly_kernel(rx_ref, near_ref, far_ref, order_ref, out_ref, *scratch)
+
+
+def butterfly(rx, lane_block, near, far, rows):
     early = lambda i: jnp.minimum(i, 3)
     late = lambda i: jnp.maximum(i - 4, 0)
-    rows = pl.pallas_call(
-        butterfly_kernel,
-        out_shape=jax.ShapeDtypeStruct((4, 8, BANDS, SLOT, HALF), jnp.bfloat16),
+    half = 0 if rows is None else 1
+    return pl.pallas_call(
+        butterfly_more_kernel if half else butterfly_kernel,
+        out_shape=jax.ShapeDtypeStruct((4, 8, BANDS, SLOT, 2 * HALF), jnp.bfloat16),
         grid=(8,),
         in_specs=[
-            pl.BlockSpec((8, ROWS, CH), lambda i: (early(i), 0, 0)),
+            pl.BlockSpec((8, ROWS, PART), lambda i: (early(i), 0, lane_block)),
             pl.BlockSpec((1, 12, PAIR, PAIR), lambda i: (early(i), 0, 0, 0)),
             pl.BlockSpec((1, 8, PAIR, PAIR), lambda i: (late(i), 0, 0, 0)),
             pl.BlockSpec((BANDS * SLOT, PAIR), lambda i: (0, 0)),
-        ],
-        out_specs=pl.BlockSpec((4, 2, BANDS, SLOT, HALF), lambda i: (0, late(i), 0, 0, 0)),
+        ] + [pl.BlockSpec(memory_space=pl.ANY)] * half,
+        out_specs=pl.BlockSpec((4, 2, BANDS, SLOT, HALF), lambda i: (0, late(i), 0, 0, half)),
         scratch_shapes=[
-            pltpu.VMEM((8, PADR, CH), jnp.bfloat16),
-            pltpu.VMEM((8, PADR, CH), jnp.bfloat16),
-            pltpu.VMEM((BLOCKS, PADR, CH), jnp.bfloat16),
-            pltpu.VMEM((2, 4, PADR, CH), jnp.bfloat16),
-        ],
+            pltpu.VMEM((8, PADR, PART), jnp.bfloat16),
+            pltpu.VMEM((8, PADR, PART), jnp.bfloat16),
+            pltpu.VMEM((BLOCKS, PADR, PART), jnp.bfloat16),
+            pltpu.VMEM((2, 4, PADR, PART), jnp.bfloat16),
+        ],
+        input_output_aliases={4: 0} if half else {},
         compiler_params=pltpu.CompilerParams(vmem_limit_bytes=56 << 20),
         name="butterfly",
-    )(rx, near, far, send_order())
-    return rows.reshape(BLOCKS * BANDS, SLOT, HALF)
+    )(rx, near, far, send_order(), *([rows] * half))
 
 
 def mirror_order():
@@ -265,14 +309,14 @@
     @pl.when(step == 0)
     def _():
         for g in range(16):
-            piece = u_ref[pl.ds(8 * g, 8)].reshape(8 * SLOT, HALF)
+            piece = u_ref[pl.ds(8 * g, 8)].reshape(8 * SLOT, PART)
             y = jnp.dot(order_ref[...], piece, preferred_element_type=jnp.float32)
             for p in range(2):
                 for r in range(5):
                     at = p * 200 + r * 40
                     v[r, pl.ds(p * 640 + 40 * g, 40), :] = y[at:at + 40].astype(jnp.bfloat16)
         for r in range(5):
-            vt[pl.ds(r * HALF, HALF), :] = v[r].T
+            vt[pl.ds(r * PART, PART), :] = v[r].T
         even, odd = sums(middle_ref[...])
         edge[...] = even - odd
 
@@ -285,12 +329,12 @@
     near = (even + odd).astype(jnp.bfloat16)
     far = (even - odd).astype(jnp.bfloat16)
     turned = jnp.dot(far, mirror_ref[...], preferred_element_type=jnp.float32)
-    lane = lax.broadcasted_iota(jnp.int32, (5 * HALF, 128), 1)
+    lane = lax.broadcasted_iota(jnp.int32, (5 * PART, 128), 1)
     head = jnp.where(lane == 0, edge[...], turned[:, :128]).astype(jnp.bfloat16)
     tail = turned[:, 128:].astype(jnp.bfloat16)
     edge[...] = far[:, :128].astype(jnp.float32)
     for r in range(5):
-        rows = slice(r * HALF, (r + 1) * HALF)
+        rows = slice(r * PART, (r + 1) * PART)
         buf[slot, 0, r] = near[rows]
         buf[slot, 1, r, :, pl.ds(0, 128)] = head[rows]
         buf[slot, 1, r, :, pl.ds(128, 128)] = tail[rows]
@@ -306,10 +350,10 @@
 def fourier(u, table):
     return pl.pallas_call(
         fourier_kernel,
-        out_shape=jax.ShapeDtypeStruct((5, HALF, NLON), jnp.bfloat16),
+        out_shape=jax.ShapeDtypeStruct((5, PART, NLON), jnp.bfloat16),
         grid=(5,),
         in_specs=[
-            pl.BlockSpec((BLOCKS * BANDS, SLOT, HALF), lambda j: (0, 0, 0)),
+            pl.BlockSpec((BLOCKS * BANDS, SLOT, PART), lambda j: (0, 0, 0)),
             pl.BlockSpec((400, 8 * SLOT), lambda j: (0, 0)),
             pl.BlockSpec((256, 256), lambda j: (0, 0)),
             pl.BlockSpec((1280, 256), lambda j: (0, 4 - j)),
@@ -317,10 +361,10 @@
         ],
         out_specs=pl.BlockSpec(memory_space=pl.ANY),
         scratch_shapes=[
-            pltpu.VMEM((5, 1280, HALF), jnp.bfloat16),
-            pltpu.VMEM((5 * HALF, 1280), jnp.bfloat16),
-            pltpu.VMEM((5 * HALF, 128), jnp.float32),
-            pltpu.VMEM((2, 2, 5, HALF, 256), jnp.bfloat16),
+            pltpu.VMEM((5, 1280, PART), jnp.bfloat16),
+            pltpu.VMEM((5 * PART, 1280), jnp.bfloat16),
+            pltpu.VMEM((5 * PART, 128), jnp.float32),
+            pltpu.VMEM((2, 2, 5, PART, 256), jnp.bfloat16),
             pltpu.SemaphoreType.DMA((2, 2)),
         ],
         compiler_params=pltpu.CompilerParams(vmem_limit_bytes=60 << 20),
@@ -341,15 +385,17 @@
 def body(coefficients, factors, wave_ids):
     wave_pos = lax.axis_index("wave")
     lev_pos = lax.axis_index("lev")
-    rf = lax.all_to_all(pack_factors(factors), "wave", 0, 0, tiled=True)
-    send_x, rf = lax.optimization_barrier((pack_coefficients(coefficients), rf))
-    rx = lax.all_to_all(send_x, "wave", 0, 0, tiled=True)
+    rx0 = lax.all_to_all(pack_first(factors, coefficients), "wave", 0, 0, tiled=True)
+    send1, rx0 = lax.optimization_barrier((pack_second(coefficients), rx0))
+    rx1 = lax.all_to_all(send1, "wave", 0, 0, tiled=True)
     own_ids = lax.dynamic_slice_in_dim(wave_ids, lev_pos * (OWN * BLOCKS) + wave_pos * OWN, OWN, 0)
     first = (own_ids[:, None] - jnp.arange(DEG, dtype=jnp.int32)[None, :]).reshape(ROWS)
     first = jnp.pad(first, (0, PADR - ROWS))
     first = jnp.broadcast_to(jnp.concatenate([first, first])[None, :], (8, PAIR))
-    near, far = section_factors(rf, first)
-    rows = butterfly(rx, near, far)
+    near, far = section_factors(rx0, first)
+    rows = butterfly(rx0, 1, near, far, None)
+    rows, rx1 = lax.optimization_barrier((rows, rx1))
+    rows = butterfly(rx1, 0, near, far, rows).reshape(BLOCKS * BANDS, SLOT, 2 * HALF)
     u = lax.all_to_all(rows, ("wave", "lev"), 0, 0, tiled=True)
     ids = wave_ids.reshape(BANDS, BLOCKS, OWN).transpose(1, 0, 2).reshape(-1)
     return fourier(u, fourier_table(ids))

time: 174 us -> 170 us (0.977)
  waiting for transfers between devices: 74.3 us -> 65.4 us
  Pallas kernels: 46.2 us -> 53.9 us
  local copies, waits for them, and re-layouts: 4.33 us -> 1.21 us
    all_to_all x2, waiting for transfers between devices: 49.4 us -> 40.4 us  [the longest x1 38.2 us: body(): lax.all_to_all(pack_first(factors, coefficients), 'wave', 0, 0, tiled=True)]
    pallas_call x4 -> x5, Pallas kernels: 39 us -> 46.6 us  [the longest x2 21.7 us: butterfly(): pl.pallas_call(butterfly_more_kernel if half else butterfly_kernel, out_s...]
    unnamed x6 -> x4, local copies, waits for them, and re-layouts: 3.13 us -> 0.01 us
    all_to_all x2, starting transfers between devices: 13 us -> 14.9 us  [the longest x1 8.6 us: body(): lax.all_to_all(pack_first(factors, coefficients), 'wave', 0, 0, tiled=True)]
  transfers between devices with their start and end apart: 3 -> 3, of which waited for: 3 -> 3; matrix products, arithmetic and copies ran while one was open for 15% -> 16% of each run, Pallas kernels for 8% -> 13%
where the time goes in v3:
time: 170 us; the launch traced here: 169 us
  waiting for transfers between devices  65.4 us (38%)
  Pallas kernels  53.9 us (32%)
  other arithmetic  25.2 us (15%)
  starting transfers between devices  23.5 us (14%)
    all_to_all x1, waiting for transfers between devices, body(): lax.all_to_all(pack_first(factors, coefficients), 'wave', 0, 0, tiled=True)  38.2 us
    all_to_all x1, waiting for transfers between devices, body(): u = lax.all_to_all(rows, ('wave', 'lev'), 0, 0, tiled=True)  25 us
    pallas_call x2, Pallas kernels, butterfly(): pl.pallas_call(butterfly_more_kernel if half else butterfly_kernel, out_s...  21.7 us
    another operation x1, other arithmetic  16.5 us
    pallas_call x1, Pallas kernels, fourier(): pl.pallas_call(fourier_kernel, out_shape=jax.ShapeDtypeStruct((5, PART, N...  14 us
    all_to_all x1, starting transfers between devices, body(): lax.all_to_all(pack_first(factors, coefficients), 'wave', 0, 0, tiled=True)  8.6 us
    all_to_all x1, starting transfers between devices, body(): u = lax.all_to_all(rows, ('wave', 'lev'), 0, 0, tiled=True)  8.52 us
    pallas_call x1, Pallas kernels, section_factors(): pl.pallas_call(section_kernel, out_shape=[jax.ShapeDtypeStruct((4, 12, PA...  7.25 us
  transfers between devices with their start and end apart: 3, of which 3 were waited for; matrix products, arithmetic and copies ran while one was open for 16% of the time, Pallas kernels for 13%

profile of v3, /device:TPU:1, one launch (start us, length us, event | category | flops | bytes accessed | tf_op | source)
XLA Modules:
  0.0 169.4 jit_solution(16348301621675851364)
XLA Ops:
  0.0 6.7 %pack_first.1 = bf16[32,100,512]{2,1,0:T(8,128)(2,1)} custom-call(bf16[5,20,20,2,160]{4,3,2,1,0:T(2,128)(2,1)} %bitcast.4, bf16[200,256]{1,0:T(8,128)(2,1)} %constant.184.clone.eye_ref, bf16[20,160,512]{2,1,0:T(8,128)(2,1)} %x_ref.1), custom_call_target="tpu_custom_call" | custom-call | tf_op jit(solution)/shard_map/pack_first/pallas_call | solution.py:99
  6.8 8.6 %all-to-all-start = ((bf16[32,100,512]{2,1,0:T(8,128)(2,1)}), bf16[32,100,512]{2,1,0:T(8,128)(2,1)S(1)}, u32[]{:S(2)}, u32[]{:S(2)}) async-start(bf16[32,100,512]{2,1,0:T(8,128)(2,1)} %pack_first.1), calls=%async_computation | async-start | bytes 6815744 | tf_op jit(solution)/shard_map/all_to_all | solution.py:388
  15.4 0.0 copy-start.1
  15.4 4.2 %pack_second.1 = bf16[32,100,256]{2,1,0:T(8,128)(2,1)} custom-call(bf16[20,160,512]{2,1,0:T(8,128)(2,1)} %x_ref.1, bf16[20,160,512]{2,1,0:T(8,128)(2,1)} %x_ref.1), custom_call_target="tpu_custom_call" | custom-call | tf_op jit(solution)/shard_map/pack_second/pallas_call | solution.py:126
  19.5 0.0 copy-done.1
  19.6 0.1 dynamic_slice.3
  19.6 0.1 iota_subtract_fusion
  19.7 0.1 sub.84
  19.8 38.2 %all-to-all-done.rf_ref.rx_ref = bf16[32,100,512]{2,1,0:T(8,128)(2,1)S(1)} async-done(((bf16[32,100,512]{2,1,0:T(8,128)(2,1)}), bf16[32,100,512]{2,1,0:T(8,128)(2,1)S(1)}, u32[]{:S(2)}, u32[]{:S(2)}) %all-to-all-start) | async-done | bytes 3276832 | tf_op jit(solution)/shard_map/all_to_all | solution.py:388
  58.0 0.0 copy-start
  58.0 6.4 %all-to-all-start.1 = ((bf16[32,100,256]{2,1,0:T(8,128)(2,1)}), bf16[32,100,256]{2,1,0:T(8,128)(2,1)}, u32[]{:S(2)}, u32[]{:S(2)}) async-start(bf16[32,100,256]{2,1,0:T(8,128)(2,1)} %pack_second.1), calls=%async_computation.1 | async-start | bytes 3407872 | tf_op jit(solution)/shard_map/all_to_all | solution.py:390
  64.4 0.1 pad_add_fusion
  64.5 0.8 fusion.54.mask_ref
  65.3 1.0 fusion.46.order_ref
  66.3 1.3 fusion.13.e_ref
  67.6 0.6 broadcast_in_dim.8.first_ref
  68.2 0.0 copy-done
  68.2 7.2 %section_factors.1 = (bf16[4,12,224,224]{3,2,1,0:T(8,128)(2,1)}, bf16[4,8,224,224]{3,2,1,0:T(8,128)(2,1)}) custom-call(bf16[32,100,512]{2,1,0:T(8,128)(2,1)} %copy-done, bf16[5,2,256,224]{3,2,1,0:T(8,128)(2,1)} %fusion.13.e_ref, f32[112,224]{1,0:T(8,128)} %fusion.54.mask_ref, s32[8,224]{1,0:T(8,128)} %broadcast_in_dim.8.first_ref), custom_call_target="tpu_custom_call" | custom-call | tf_op jit(solution)/shard_map/section_factors/pallas_call | solution.py:186
  75.5 10.8 %butterfly.2.rows_ref = bf16[4,8,4,56,256]{4,3,2,1,0:T(8,128)(2,1)} custom-call(bf16[32,100,512]{2,1,0:T(8,128)(2,1)} %copy-done, bf16[4,12,224,224]{3,2,1,0:T(8,128)(2,1)} %get-tuple-element.12.near_ref, bf16[4,8,224,224]{3,2,1,0:T(8,128)(2,1)} %get-tuple-element.13.far_ref, bf16[224,224]{1,0:T(8,128)(2,1)} %fusion.46.order_ref), custom_call_target="tpu_custom_call" | custom-call | tf_op jit(solution)/shard_map/butterfly/pallas_call | solution.py:265
  86.3 2.2 %all-to-all-done.1.rx_ref = bf16[32,100,256]{2,1,0:T(8,128)(2,1)} async-done(((bf16[32,100,256]{2,1,0:T(8,128)(2,1)}), bf16[32,100,256]{2,1,0:T(8,128)(2,1)}, u32[]{:S(2)}, u32[]{:S(2)}) %all-to-all-start.1) | async-done | bytes 1638432 | tf_op jit(solution)/shard_map/all_to_all | solution.py:390
  88.5 10.8 %butterfly.3 = bf16[4,8,4,56,256]{4,3,2,1,0:T(8,128)(2,1)} custom-call(bf16[32,100,256]{2,1,0:T(8,128)(2,1)} %all-to-all-done.1.rx_ref, bf16[4,12,224,224]{3,2,1,0:T(8,128)(2,1)} %get-tuple-element.12.near_ref, bf16[4,8,224,224]{3,2,1,0:T(8,128)(2,1)} %get-tuple-element.13.far_ref, ...), custom_call_target="tpu_custom_call", output_to_operand_aliasing={{}: (4, {})} | custom-call | tf_op jit(solution)/shard_map/butterfly/pallas_call | solution.py:265
  99.3 8.5 %all-to-all-start.2 = ((bf16[128,56,256]{2,1,0:T(8,128)(2,1)}), bf16[128,56,256]{2,1,0:T(8,128)(2,1)}, u32[]{:S(2)}, u32[]{:S(2)}) async-start(bf16[128,56,256]{2,1,0:T(8,128)(2,1)} %bitcast.3), calls=%async_computation.2 | async-start | bytes 7340032 | tf_op jit(solution)/shard_map/all_to_all | solution.py:399
  107.9 0.2 reshape.29
  108.1 0.2 reshape.30
  108.4 0.7 fusion.30.mirror_ref
  109.1 2.5 %fusion.24.order_ref = bf16[400,448]{1,0:T(8,128)(2,1)} fusion(s32[400]{0:T(512)S(1)} %get-tuple-element.37, s32[400]{0:T(512)S(1)} %get-tuple-element.47, s32[400]{0:T(512)S(1)} %get-tuple-element.38, s32[400]{0:T(512)S(1)} %get-tuple-element.42, s32[400]{0:T(512)S(1)} %get-tuple-element.39, s32[400]{0:T(512)S(1)} %get-tuple-element.48, ...), kind=kLoop, calls=%fused_computation.38 | loop fusion | flops 4659200 | bytes 372800 | tf_op jit(solution)/shard_map/convert_element_type | solution.py:146
  111.6 16.5 %multiply_convert_fusion.1 = (bf16[640,1408]{1,0:T(8,128)(2,1)S(1)}, bf16[640,1408]{1,0:T(8,128)(2,1)S(1)}) fusion(s32[640]{0:T(1024)S(1)} %reshape.30, f32[640]{0:T(1024)S(1)} %get-tuple-element.19, f32[640]{0:T(1024)S(1)} %get-tuple-element.20), kind=kLoop, calls=%fused_computation.10 | loop fusion | flops 11714560 | bytes 3612160 | tf_op jit(solution)/shard_map/convert
  128.1 2.2 %pad_maximum_fusion.table_ref.middle_ref = bf16[1280,1408]{1,0:T(8,128)(2,1)} fusion(bf16[640,1408]{1,0:T(8,128)(2,1)S(1)} %get-tuple-element.18, bf16[640,1408]{1,0:T(8,128)(2,1)S(1)} %get-tuple-element.17), kind=kLoop, calls=%fused_computation.8 | loop fusion | flops 7208960 | bytes 7208960 | tf_op jit(solution)/shard_map/concatenate | solution.py:382
  130.3 25.0 %all-to-all-done.2.u_ref = bf16[128,56,256]{2,1,0:T(8,128)(2,1)} async-done(((bf16[128,56,256]{2,1,0:T(8,128)(2,1)}), bf16[128,56,256]{2,1,0:T(8,128)(2,1)}, u32[]{:S(2)}, u32[]{:S(2)}) %all-to-all-start.2) | async-done | bytes 3670048 | tf_op jit(solution)/shard_map/all_to_all | solution.py:399
  155.3 14.0 %fourier.1 = bf16[5,256,2560]{2,1,0:T(8,128)(2,1)} custom-call(bf16[128,56,256]{2,1,0:T(8,128)(2,1)} %all-to-all-done.2.u_ref, bf16[400,448]{1,0:T(8,128)(2,1)} %fusion.24.order_ref, bf16[256,256]{1,0:T(8,128)(2,1)} %fusion.30.mirror_ref, bf16[1280,1408]{1,0:T(8,128)(2,1)} %pad_maximum_fusion.table_ref.middle_ref, ...), custom_call_target="tpu_custom_call" | custom-call | tf_op jit(solution)/shard_map/fourier/pallas_call | solution.py:351
  (18 shorter events, 0.2 us)
Async XLA Ops:
  6.8 51.3 %all-to-all-start = ((bf16[32,100,512]{2,1,0:T(8,128)(2,1)}), bf16[32,100,512]{2,1,0:T(8,128)(2,1)S(1)}, u32[]{:S(2)}, u32[]{:S(2)}) async-start(bf16[32,100,512]{2,1,0:T(8,128)(2,1)} %pack_first.1), calls=%async_computation | async-start | bytes 6815744 | tf_op jit(solution)/shard_map/all_to_all | solution.py:388
  15.4 4.2 %copy-start.1 = (s32[640]{0:T(1024)S(1)}, s32[640]{0:T(1024)}, u32[]{:S(2)}) copy-start(s32[640]{0:T(1024)} %param.6) | copy-start | bytes 7684
  58.0 10.2 %copy-start = (bf16[32,100,512]{2,1,0:T(8,128)(2,1)}, bf16[32,100,512]{2,1,0:T(8,128)(2,1)S(1)}, u32[]{:S(2)}) copy-start(bf16[32,100,512]{2,1,0:T(8,128)(2,1)S(1)} %all-to-all-done.rf_ref.rx_ref) | copy-start | bytes 9830404
  58.0 30.5 %all-to-all-start.1 = ((bf16[32,100,256]{2,1,0:T(8,128)(2,1)}), bf16[32,100,256]{2,1,0:T(8,128)(2,1)}, u32[]{:S(2)}, u32[]{:S(2)}) async-start(bf16[32,100,256]{2,1,0:T(8,128)(2,1)} %pack_second.1), calls=%async_computation.1 | async-start | bytes 3407872 | tf_op jit(solution)/shard_map/all_to_all | solution.py:390
  99.3 55.9 %all-to-all-start.2 = ((bf16[128,56,256]{2,1,0:T(8,128)(2,1)}), bf16[128,56,256]{2,1,0:T(8,128)(2,1)}, u32[]{:S(2)}, u32[]{:S(2)}) async-start(bf16[128,56,256]{2,1,0:T(8,128)(2,1)} %bitcast.3), calls=%async_computation.2 | async-start | bytes 7340032 | tf_op jit(solution)/shard_map/all_to_all | solution.py:399

commit v4 on v3

--- a/solution.py
+++ b/solution.py
@@ -1,3 +1,4 @@
+import functools
 import math
 
 import jax
@@ -206,78 +207,109 @@
     )(rf, select_matrices(), diagonal_mask(), first)
 
 
-def butterfly_kernel(rx_ref, near_ref, far_ref, order_ref, out_ref, xa, xb, xc, xd):
-    step = pl.program_id(0)
-
-    @pl.when(step == 0)
-    def _():
-        for b in range(8):
-            xa[b, pl.ds(96, 16), :] = jnp.zeros((16, PART), jnp.bfloat16)
-
-    @pl.when(step < 4)
-    def _():
-        for b in range(8):
-            xa[b, pl.ds(0, ROWS), :] = rx_ref[b]
+def butterfly_kernel(half, lane_block, rx_ref, near_ref, far_ref, order_ref, *refs):
+    out_ref, rs, ns, fs, stage, xa, xb, xc, xd, rsem, nsem, fsem, osem = refs[-13:]
+
+    def load_rows(g):
+        rows = rx_ref.at[pl.ds(8 * g, 8), :, pl.ds(PART * lane_block, PART)]
+        return pltpu.make_async_copy(rows, rs.at[pl.ds(8 * g, 8)], rsem.at[g])
+
+    def load_near(g, s):
+        return pltpu.make_async_copy(near_ref.at[g, pl.ds(4 * s, 4)], ns.at[g, pl.ds(4 * s, 4)], nsem.at[g, s])
+
+    def load_far(t):
+        return pltpu.make_async_copy(far_ref.at[t], fs.at[t], fsem.at[t])
+
+    def store(t):
+        rows = out_ref.at[:, pl.ds(2 * t, 2), :, :, pl.ds(HALF * half, HALF)]
+        return pltpu.make_async_copy(stage.at[:, pl.ds(2 * t, 2)], rows, osem.at[t])
+
+    for g in range(4):
+        load_rows(g).start()
+        for s in range(3):
+            load_near(g, s).start()
+    for t in range(4):
+        load_far(t).start()
+    for b in range(16):
+        xa[b, pl.ds(96, 16), :] = jnp.zeros((16, PART), jnp.bfloat16)
+
+    def early(i, carry):
+        for q in range(2):
+            load_rows(2 * i + q).wait()
+            for b in range(8):
+                xa[8 * q + b, pl.ds(0, ROWS), :] = rs[16 * i + 8 * q + b]
         src, dst = xa, xb
         for s in range(3):
-            base = 8 * step if s == 2 else 0
+            base = 16 * i if s == 2 else 0
             out = xc if s == 2 else dst
+            for q in range(2):
+                load_near(2 * i + q, s).wait()
+            for q in range(2):
+                for j in range(4):
+                    low = lower_block(s, q, j)
+                    high = low + (1 << s)
+                    right = jnp.concatenate([src[low], src[high]], axis=0)
+                    y = jnp.dot(ns[2 * i + q, 4 * s + j], right, preferred_element_type=jnp.float32)
+                    y = y.astype(jnp.bfloat16)
+                    out[base + low] = y[:PADR]
+                    out[base + high] = y[PADR:]
+            src, dst = dst, src
+        return carry
+
+    lax.fori_loop(0, 2, early, 0)
+
+    def late(i, carry):
+        for q in range(2):
+            load_far(2 * i + q).wait()
+        for q in range(2):
             for j in range(4):
-                low = lower_block(s, 0, j)
-                high = low + (1 << s)
-                right = jnp.concatenate([src[low], src[high]], axis=0)
-                y = jnp.dot(near_ref[0, 4 * s + j], right, preferred_element_type=jnp.float32).astype(jnp.bfloat16)
-                out[base + low] = y[:PADR]
-                out[base + high] = y[PADR:]
-            src, dst = dst, src
-
-    @pl.when(step >= 4)
-    def _():
-        first = 2 * (step - 4)
-        for j in range(4):
-            r, h = j // 2, j % 2
-            low = first + r + 16 * h
-            right = jnp.concatenate([xc[low], xc[low + 8]], axis=0)
-            y = jnp.dot(far_ref[0, j], right, preferred_element_type=jnp.float32).astype(jnp.bfloat16)
-            xd[r, 2 * h] = y[:PADR]
-            xd[r, 2 * h + 1] = y[PADR:]
-        for j in range(4):
-            r, h = j // 2, j % 2
-            right = jnp.concatenate([xd[r, h], xd[r, h + 2]], axis=0)
-            y = jnp.dot(far_ref[0, 4 + j], right, preferred_element_type=jnp.float32).astype(jnp.bfloat16)
-            re = jnp.concatenate([y[:PADR, :HALF], y[PADR:, :HALF]], axis=1)
-            im = jnp.concatenate([y[:PADR, HALF:], y[PADR:, HALF:]], axis=1)
-            z = jnp.dot(order_ref[...], jnp.concatenate([re, im], axis=0), preferred_element_type=jnp.float32)
-            for half in range(2):
-                for band in range(BANDS):
-                    piece = z[band * SLOT:(band + 1) * SLOT, half * HALF:(half + 1) * HALF]
-                    out_ref[h + 2 * half, r, band] = piece.astype(jnp.bfloat16)
-
-
-def butterfly_more_kernel(rx_ref, near_ref, far_ref, order_ref, rows_ref, out_ref, *scratch):
-    butterfly_kernel(rx_ref, near_ref, far_ref, order_ref, out_ref, *scratch)
+                r, h = j // 2, j % 2
+                low = 4 * i + 2 * q + r + 16 * h
+                right = jnp.concatenate([xc[low], xc[low + 8]], axis=0)
+                y = jnp.dot(fs[2 * i + q, j], right, preferred_element_type=jnp.float32).astype(jnp.bfloat16)
+                xd[2 * q + r, 2 * h] = y[:PADR]
+                xd[2 * q + r, 2 * h + 1] = y[PADR:]
+        for q in range(2):
+            for j in range(4):
+                r, h = j // 2, j % 2
+                right = jnp.concatenate([xd[2 * q + r, h], xd[2 * q + r, h + 2]], axis=0)
+                y = jnp.dot(fs[2 * i + q, 4 + j], right, preferred_element_type=jnp.float32).astype(jnp.bfloat16)
+                re = jnp.concatenate([y[:PADR, :HALF], y[PADR:, :HALF]], axis=1)
+                im = jnp.concatenate([y[:PADR, HALF:], y[PADR:, HALF:]], axis=1)
+                z = jnp.dot(order_ref[...], jnp.concatenate([re, im], axis=0), preferred_element_type=jnp.float32)
+                for k in range(2):
+                    for band in range(BANDS):
+                        piece = z[band * SLOT:(band + 1) * SLOT, k * HALF:(k + 1) * HALF]
+                        stage[h + 2 * k, 4 * i + 2 * q + r, band] = piece.astype(jnp.bfloat16)
+            store(2 * i + q).start()
+        return carry
+
+    lax.fori_loop(0, 2, late, 0)
+    for t in range(4):
+        store(t).wait()
 
 
 def butterfly(rx, lane_block, near, far, rows):
-    early = lambda i: jnp.minimum(i, 3)
-    late = lambda i: jnp.maximum(i - 4, 0)
     half = 0 if rows is None else 1
+    anywhere = pl.BlockSpec(memory_space=pl.ANY)
     return pl.pallas_call(
-        butterfly_more_kernel if half else butterfly_kernel,
+        functools.partial(butterfly_kernel, half, lane_block),
         out_shape=jax.ShapeDtypeStruct((4, 8, BANDS, SLOT, 2 * HALF), jnp.bfloat16),
-        grid=(8,),
-        in_specs=[
-            pl.BlockSpec((8, ROWS, PART), lambda i: (early(i), 0, lane_block)),
-            pl.BlockSpec((1, 12, PAIR, PAIR), lambda i: (early(i), 0, 0, 0)),
-            pl.BlockSpec((1, 8, PAIR, PAIR), lambda i: (late(i), 0, 0, 0)),
-            pl.BlockSpec((BANDS * SLOT, PAIR), lambda i: (0, 0)),
-        ] + [pl.BlockSpec(memory_space=pl.ANY)] * half,
-        out_specs=pl.BlockSpec((4, 2, BANDS, SLOT, HALF), lambda i: (0, late(i), 0, 0, half)),
+        in_specs=[anywhere, anywhere, anywhere, pl.BlockSpec(memory_space=pltpu.VMEM)] + [anywhere] * half,
+        out_specs=anywhere,
         scratch_shapes=[
-            pltpu.VMEM((8, PADR, PART), jnp.bfloat16),
-            pltpu.VMEM((8, PADR, PART), jnp.bfloat16),
+            pltpu.VMEM((BLOCKS, ROWS, PART), jnp.bfloat16),
+            pltpu.VMEM((4, 12, PAIR, PAIR), jnp.bfloat16),
+            pltpu.VMEM((4, 8, PAIR, PAIR), jnp.bfloat16),
+            pltpu.VMEM((4, 8, BANDS, SLOT, HALF), jnp.bfloat16),
+            pltpu.VMEM((16, PADR, PART), jnp.bfloat16),
+            pltpu.VMEM((16, PADR, PART), jnp.bfloat16),
             pltpu.VMEM((BLOCKS, PADR, PART), jnp.bfloat16),
-            pltpu.VMEM((2, 4, PADR, PART), jnp.bfloat16),
+            pltpu.VMEM((4, 4, PADR, PART), jnp.bfloat16),
+            pltpu.SemaphoreType.DMA((4,)),
+            pltpu.SemaphoreType.DMA((4, 3)),
+            pltpu.SemaphoreType.DMA((4,)),
+            pltpu.SemaphoreType.DMA((4,)),
         ],
         input_output_aliases={4: 0} if half else {},
         compiler_params=pltpu.CompilerParams(vmem_limit_bytes=56 << 20),

time: 170 us -> 168 us (0.988)
  Pallas kernels: 53.9 us -> 51.9 us
    pallas_call x2, Pallas kernels: 21.7 us -> 19.7 us  [butterfly(): pl.pallas_call(functools.partial(butterfly_kernel, half, lane_block), out...]
where the time goes in v4:
time: 168 us
  waiting for transfers between devices  66.3 us (39%)
  Pallas kernels  51.9 us (31%)
  other arithmetic  25.2 us (15%)
  starting transfers between devices  22.5 us (13%)
    all_to_all x1, waiting for transfers between devices, body(): lax.all_to_all(pack_first(factors, coefficients), 'wave', 0, 0, tiled=True)  38.2 us
    all_to_all x1, waiting for transfers between devices, body(): u = lax.all_to_all(rows, ('wave', 'lev'), 0, 0, tiled=True)  25 us
    pallas_call x2, Pallas kernels, butterfly(): pl.pallas_call(functools.partial(butterfly_kernel, half, lane_block), out...  19.7 us
    another operation x1, other arithmetic  16.5 us
    pallas_call x1, Pallas kernels, fourier(): pl.pallas_call(fourier_kernel, out_shape=jax.ShapeDtypeStruct((5, PART, N...  14 us
    all_to_all x1, starting transfers between devices, body(): lax.all_to_all(pack_first(factors, coefficients), 'wave', 0, 0, tiled=True)  8.6 us
    all_to_all x1, starting transfers between devices, body(): u = lax.all_to_all(rows, ('wave', 'lev'), 0, 0, tiled=True)  7.55 us
    pallas_call x1, Pallas kernels, section_factors(): pl.pallas_call(section_kernel, out_shape=[jax.ShapeDtypeStruct((4, 12, PA...  7.24 us
  transfers between devices with their start and end apart: 3, of which 3 were waited for; matrix products, arithmetic and copies ran while one was open for 16% of the time, Pallas kernels for 13%

profile of v4, /device:TPU:1, one launch (start us, length us, event | category | flops | bytes accessed | tf_op | source)
XLA Modules:
  0.0 167.5 jit_solution(1193874289358907862)
XLA Ops:
  0.0 6.7 %pack_first.1 = bf16[32,100,512]{2,1,0:T(8,128)(2,1)} custom-call(bf16[5,20,20,2,160]{4,3,2,1,0:T(2,128)(2,1)} %bitcast.4, bf16[200,256]{1,0:T(8,128)(2,1)} %constant.184.clone.eye_ref, bf16[20,160,512]{2,1,0:T(8,128)(2,1)} %x_ref.1), custom_call_target="tpu_custom_call" | custom-call | tf_op jit(solution)/shard_map/pack_first/pallas_call | solution.py:100
  6.8 8.6 %all-to-all-start = ((bf16[32,100,512]{2,1,0:T(8,128)(2,1)}), bf16[32,100,512]{2,1,0:T(8,128)(2,1)S(1)}, u32[]{:S(2)}, u32[]{:S(2)}) async-start(bf16[32,100,512]{2,1,0:T(8,128)(2,1)} %pack_first.1), calls=%async_computation | async-start | bytes 6815744 | tf_op jit(solution)/shard_map/all_to_all | solution.py:420
  15.4 0.0 copy-start.1
  15.4 4.2 %pack_second.1 = bf16[32,100,256]{2,1,0:T(8,128)(2,1)} custom-call(bf16[20,160,512]{2,1,0:T(8,128)(2,1)} %x_ref.1, bf16[20,160,512]{2,1,0:T(8,128)(2,1)} %x_ref.1), custom_call_target="tpu_custom_call" | custom-call | tf_op jit(solution)/shard_map/pack_second/pallas_call | solution.py:127
  19.5 0.0 copy-done.1
  19.6 0.1 dynamic_slice.3
  19.6 0.1 iota_subtract_fusion
  19.7 0.1 sub.84
  19.8 38.2 %all-to-all-done.rf_ref.rx_ref = bf16[32,100,512]{2,1,0:T(8,128)(2,1)S(1)} async-done(((bf16[32,100,512]{2,1,0:T(8,128)(2,1)}), bf16[32,100,512]{2,1,0:T(8,128)(2,1)S(1)}, u32[]{:S(2)}, u32[]{:S(2)}) %all-to-all-start) | async-done | bytes 3276832 | tf_op jit(solution)/shard_map/all_to_all | solution.py:420
  58.0 0.0 copy-start
  58.0 6.4 %all-to-all-start.1 = ((bf16[32,100,256]{2,1,0:T(8,128)(2,1)}), bf16[32,100,256]{2,1,0:T(8,128)(2,1)}, u32[]{:S(2)}, u32[]{:S(2)}) async-start(bf16[32,100,256]{2,1,0:T(8,128)(2,1)} %pack_second.1), calls=%async_computation.1 | async-start | bytes 3407872 | tf_op jit(solution)/shard_map/all_to_all | solution.py:422
  64.4 0.1 pad_add_fusion
  64.5 0.8 fusion.54.mask_ref
  65.3 1.0 fusion.46.order_ref
  66.3 1.3 fusion.13.e_ref
  67.6 0.6 broadcast_in_dim.8.first_ref
  68.2 0.0 copy-done
  68.2 7.2 %section_factors.1 = (bf16[4,12,224,224]{3,2,1,0:T(8,128)(2,1)}, bf16[4,8,224,224]{3,2,1,0:T(8,128)(2,1)}) custom-call(bf16[32,100,512]{2,1,0:T(8,128)(2,1)} %copy-done, bf16[5,2,256,224]{3,2,1,0:T(8,128)(2,1)} %fusion.13.e_ref, f32[112,224]{1,0:T(8,128)} %fusion.54.mask_ref, s32[8,224]{1,0:T(8,128)} %broadcast_in_dim.8.first_ref), custom_call_target="tpu_custom_call" | custom-call | tf_op jit(solution)/shard_map/section_factors/pallas_call | solution.py:187
  75.5 9.8 %butterfly.2.refs_0_ = bf16[4,8,4,56,256]{4,3,2,1,0:T(8,128)(2,1)} custom-call(bf16[32,100,512]{2,1,0:T(8,128)(2,1)} %copy-done, bf16[4,12,224,224]{3,2,1,0:T(8,128)(2,1)} %get-tuple-element.12.near_ref, bf16[4,8,224,224]{3,2,1,0:T(8,128)(2,1)} %get-tuple-element.13.far_ref, bf16[224,224]{1,0:T(8,128)(2,1)} %fusion.46.order_ref), custom_call_target="tpu_custom_call" | custom-call | tf_op jit(solution)/shard_map/butterfly/pallas_call | solution.py:295
  85.3 3.2 %all-to-all-done.1.rx_ref = bf16[32,100,256]{2,1,0:T(8,128)(2,1)} async-done(((bf16[32,100,256]{2,1,0:T(8,128)(2,1)}), bf16[32,100,256]{2,1,0:T(8,128)(2,1)}, u32[]{:S(2)}, u32[]{:S(2)}) %all-to-all-start.1) | async-done | bytes 1638432 | tf_op jit(solution)/shard_map/all_to_all | solution.py:422
  88.5 9.8 %butterfly.3 = bf16[4,8,4,56,256]{4,3,2,1,0:T(8,128)(2,1)} custom-call(bf16[32,100,256]{2,1,0:T(8,128)(2,1)} %all-to-all-done.1.rx_ref, bf16[4,12,224,224]{3,2,1,0:T(8,128)(2,1)} %get-tuple-element.12.near_ref, bf16[4,8,224,224]{3,2,1,0:T(8,128)(2,1)} %get-tuple-element.13.far_ref, ...), custom_call_target="tpu_custom_call", output_to_operand_aliasing={{}: (4, {})} | custom-call | tf_op jit(solution)/shard_map/butterfly/pallas_call | solution.py:295
  98.4 7.6 %all-to-all-start.2 = ((bf16[128,56,256]{2,1,0:T(8,128)(2,1)}), bf16[128,56,256]{2,1,0:T(8,128)(2,1)}, u32[]{:S(2)}, u32[]{:S(2)}) async-start(bf16[128,56,256]{2,1,0:T(8,128)(2,1)} %bitcast.3), calls=%async_computation.2 | async-start | bytes 7340032 | tf_op jit(solution)/shard_map/all_to_all | solution.py:431
  105.9 0.2 reshape.29
  106.2 0.2 reshape.30
  106.5 0.7 fusion.30.mirror_ref
  107.1 2.5 %fusion.24.order_ref = bf16[400,448]{1,0:T(8,128)(2,1)} fusion(s32[400]{0:T(512)S(1)} %get-tuple-element.37, s32[400]{0:T(512)S(1)} %get-tuple-element.47, s32[400]{0:T(512)S(1)} %get-tuple-element.38, s32[400]{0:T(512)S(1)} %get-tuple-element.42, s32[400]{0:T(512)S(1)} %get-tuple-element.39, s32[400]{0:T(512)S(1)} %get-tuple-element.48, ...), kind=kLoop, calls=%fused_computation.38 | loop fusion | flops 4659200 | bytes 372800 | tf_op jit(solution)/shard_map/convert_element_type | solution.py:147
  109.6 16.5 %multiply_convert_fusion.1 = (bf16[640,1408]{1,0:T(8,128)(2,1)S(1)}, bf16[640,1408]{1,0:T(8,128)(2,1)S(1)}) fusion(s32[640]{0:T(1024)S(1)} %reshape.30, f32[640]{0:T(1024)S(1)} %get-tuple-element.19, f32[640]{0:T(1024)S(1)} %get-tuple-element.20), kind=kLoop, calls=%fused_computation.10 | loop fusion | flops 11714560 | bytes 3612160 | tf_op jit(solution)/shard_map/convert
  126.2 2.2 %pad_maximum_fusion.table_ref.middle_ref = bf16[1280,1408]{1,0:T(8,128)(2,1)} fusion(bf16[640,1408]{1,0:T(8,128)(2,1)S(1)} %get-tuple-element.18, bf16[640,1408]{1,0:T(8,128)(2,1)S(1)} %get-tuple-element.17), kind=kLoop, calls=%fused_computation.8 | loop fusion | flops 7208960 | bytes 7208960 | tf_op jit(solution)/shard_map/concatenate | solution.py:414
  128.3 25.0 %all-to-all-done.2.u_ref = bf16[128,56,256]{2,1,0:T(8,128)(2,1)} async-done(((bf16[128,56,256]{2,1,0:T(8,128)(2,1)}), bf16[128,56,256]{2,1,0:T(8,128)(2,1)}, u32[]{:S(2)}, u32[]{:S(2)}) %all-to-all-start.2) | async-done | bytes 3670048 | tf_op jit(solution)/shard_map/all_to_all | solution.py:431
  153.3 14.0 %fourier.1 = bf16[5,256,2560]{2,1,0:T(8,128)(2,1)} custom-call(bf16[128,56,256]{2,1,0:T(8,128)(2,1)} %all-to-all-done.2.u_ref, bf16[400,448]{1,0:T(8,128)(2,1)} %fusion.24.order_ref, bf16[256,256]{1,0:T(8,128)(2,1)} %fusion.30.mirror_ref, bf16[1280,1408]{1,0:T(8,128)(2,1)} %pad_maximum_fusion.table_ref.middle_ref, ...), custom_call_target="tpu_custom_call" | custom-call | tf_op jit(solution)/shard_map/fourier/pallas_call | solution.py:383
  (18 shorter events, 0.2 us)
Async XLA Ops:
  6.8 51.3 %all-to-all-start = ((bf16[32,100,512]{2,1,0:T(8,128)(2,1)}), bf16[32,100,512]{2,1,0:T(8,128)(2,1)S(1)}, u32[]{:S(2)}, u32[]{:S(2)}) async-start(bf16[32,100,512]{2,1,0:T(8,128)(2,1)} %pack_first.1), calls=%async_computation | async-start | bytes 6815744 | tf_op jit(solution)/shard_map/all_to_all | solution.py:420
  15.4 4.2 %copy-start.1 = (s32[640]{0:T(1024)S(1)}, s32[640]{0:T(1024)}, u32[]{:S(2)}) copy-start(s32[640]{0:T(1024)} %param.6) | copy-start | bytes 7684
  58.0 10.2 %copy-start = (bf16[32,100,512]{2,1,0:T(8,128)(2,1)}, bf16[32,100,512]{2,1,0:T(8,128)(2,1)S(1)}, u32[]{:S(2)}) copy-start(bf16[32,100,512]{2,1,0:T(8,128)(2,1)S(1)} %all-to-all-done.rf_ref.rx_ref) | copy-start | bytes 9830404
  58.0 30.5 %all-to-all-start.1 = ((bf16[32,100,256]{2,1,0:T(8,128)(2,1)}), bf16[32,100,256]{2,1,0:T(8,128)(2,1)}, u32[]{:S(2)}, u32[]{:S(2)}) async-start(bf16[32,100,256]{2,1,0:T(8,128)(2,1)} %pack_second.1), calls=%async_computation.1 | async-start | bytes 3407872 | tf_op jit(solution)/shard_map/all_to_all | solution.py:422
  98.4 54.9 %all-to-all-start.2 = ((bf16[128,56,256]{2,1,0:T(8,128)(2,1)}), bf16[128,56,256]{2,1,0:T(8,128)(2,1)}, u32[]{:S(2)}, u32[]{:S(2)}) async-start(bf16[128,56,256]{2,1,0:T(8,128)(2,1)} %bitcast.3), calls=%async_computation.2 | async-start | bytes 7340032 | tf_op jit(solution)/shard_map/all_to_all | solution.py:431

commit v5 on v4

--- a/solution.py
+++ b/solution.py
@@ -22,6 +22,8 @@
 PADR = 112
 SLOT = 56
 PAIR = 2 * PADR
+XROWS = 104
+FROWS = 80
 
 
 def select_matrices():
@@ -62,77 +64,115 @@
         order[v] = (ahead == 4 * v).astype(jnp.float32).astype(jnp.bfloat16)
 
 
-def pack_rows(srcs, order, out_ref):
+def fold_lanes():
+    f = np.zeros((256, 512), np.float32)
+    for q in range(4):
+        for j in range(50):
+            f[50 * q + j, 128 * q + 72 + j] = 1
+    return f
+
+
+def fold_rows():
+    f = np.zeros((FROWS, 96), np.float32)
+    for q in range(4):
+        for o in range(DEG):
+            row = 16 * q + o if o < 16 else 64 + 4 * q + o - 16
+            f[row, 24 * q + o] = 1
+    return f
+
+
+def chosen_rows(srcs, order, group):
+    start = 4 * OWN * group
+    at = start // 16 * 16
+    window = jnp.concatenate([src[:, at:at + 32, :].reshape(DEG * 32, src.shape[2]) for src in srcs], axis=1)
+    return jnp.dot(order[(start - at) // 4], window, preferred_element_type=jnp.float32)
+
+
+def pack_rows(srcs, order, out_ref, first):
     for group in range(BLOCKS // 4):
-        start = 4 * OWN * group
-        at = start // 16 * 16
-        window = jnp.concatenate([src[:, at:at + 32, :].reshape(DEG * 32, src.shape[2]) for src in srcs], axis=1)
-        y = jnp.dot(order[(start - at) // 4], window, preferred_element_type=jnp.float32)
+        y = chosen_rows(srcs, order, group)
         for d in range(4):
-            out_ref[4 * group + d] = y[104 * d:104 * d + ROWS].astype(jnp.bfloat16)
-
-
-def pack_first_kernel(f_ref, eye_ref, x_ref, out_ref, turned, order, xs, sem):
+            out_ref[4 * group + d, pl.ds(first, XROWS), :] = y[XROWS * d:XROWS * (d + 1)].astype(jnp.bfloat16)
+
+
+def pack_folded(src, order, lanes_ref, out_ref):
+    for group in range(BLOCKS // 4):
+        y = chosen_rows([src], order, group)
+        rest = [y[XROWS * d + FROWS:XROWS * (d + 1)].astype(jnp.bfloat16) for d in range(4)]
+        wide = jnp.dot(jnp.concatenate(rest, axis=0), lanes_ref[...], preferred_element_type=jnp.float32)
+        for d in range(4):
+            part = [wide[24 * d:24 * (d + 1), 128 * q:128 * (q + 1)] for q in range(4)]
+            ends = [part[q][16:] + pltpu.roll(part[q + 1][16:], 4, 0) for q in (0, 2)]
+            spare = jnp.concatenate([part[q][:16] for q in range(4)] + ends, axis=0)
+            own = y[XROWS * d:XROWS * d + FROWS]
+            out_ref[4 * group + d, pl.ds(0, FROWS), pl.ds(0, 128)] = own[:, :128].astype(jnp.bfloat16)
+            out_ref[4 * group + d, pl.ds(0, FROWS), pl.ds(128, 128)] = (own[:, 128:] + spare).astype(jnp.bfloat16)
+
+
+def pack_first_kernel(f_ref, eye_ref, lanes_ref, x_ref, out_ref, turned, order, xs, stage, sem, osem):
     fetch = [
         pltpu.make_async_copy(x_ref.at[:, :, pl.ds(p * PART, HALF)], xs.at[:, :, pl.ds(p * HALF, HALF)], sem.at[p])
         for p in range(2)
     ]
-
-    @pl.when(pl.program_id(0) == 0)
-    def _():
-        for copy in fetch:
-            copy.start()
-        fill_pack_order(order)
-        for o in range(DEG):
-            left = jnp.concatenate([f_ref[s, o].reshape(2 * DEG, OWN * BLOCKS) for s in range(SECTIONS)], axis=0)
-            y = lax.dot_general(left, eye_ref[...], (((0,), (0,)), ((), ())), preferred_element_type=jnp.float32)
-            turned[o] = y.astype(jnp.bfloat16)
-        pack_rows([turned], order, out_ref)
-
-    @pl.when(pl.program_id(0) == 1)
-    def _():
-        for copy in fetch:
-            copy.wait()
-        pack_rows([xs], order, out_ref)
+    for copy in fetch:
+        copy.start()
+    fill_pack_order(order)
+    for o in range(DEG):
+        left = jnp.concatenate([f_ref[s, o].reshape(2 * DEG, OWN * BLOCKS) for s in range(SECTIONS)], axis=0)
+        y = lax.dot_general(left, eye_ref[...], (((0,), (0,)), ((), ())), preferred_element_type=jnp.float32)
+        turned[o] = y.astype(jnp.bfloat16)
+    pack_folded(turned, order, lanes_ref, stage)
+    pieces = [pl.ds(0, FROWS), pl.ds(FROWS, XROWS)]
+    store = [pltpu.make_async_copy(stage.at[:, at, :], out_ref.at[:, at, :], osem.at[i]) for i, at in enumerate(pieces)]
+    store[0].start()
+    for copy in fetch:
+        copy.wait()
+    pack_rows([xs], order, stage, FROWS)
+    store[1].start()
+    for copy in store:
+        copy.wait()
 
 
 def pack_first(factors, x):
+    here = pl.BlockSpec(memory_space=pltpu.VMEM)
     return pl.pallas_call(
         pack_first_kernel,
-        out_shape=jax.ShapeDtypeStruct((BLOCKS, ROWS, 2 * PART), jnp.bfloat16),
-        grid=(2,),
-        in_specs=[
-            pl.BlockSpec((SECTIONS, DEG, DEG, 2, OWN * BLOCKS), lambda i: (0, 0, 0, 0, 0)),
-            pl.BlockSpec((200, 256), lambda i: (0, 0)),
-            pl.BlockSpec(memory_space=pl.ANY),
-        ],
-        out_specs=pl.BlockSpec((BLOCKS, ROWS, PART), lambda i: (0, 0, i)),
+        out_shape=jax.ShapeDtypeStruct((BLOCKS, FROWS + XROWS, PART), jnp.bfloat16),
+        in_specs=[here, here, here, pl.BlockSpec(memory_space=pl.ANY)],
+        out_specs=pl.BlockSpec(memory_space=pl.ANY),
         scratch_shapes=[
             pltpu.VMEM((DEG, OWN * BLOCKS, 256), jnp.bfloat16),
             pltpu.VMEM((4, 416, 640), jnp.bfloat16),
             pltpu.VMEM((DEG, OWN * BLOCKS, PART), jnp.bfloat16),
+            pltpu.VMEM((BLOCKS, FROWS + XROWS, PART), jnp.bfloat16),
+            pltpu.SemaphoreType.DMA((2,)),
             pltpu.SemaphoreType.DMA((2,)),
         ],
         compiler_params=pltpu.CompilerParams(vmem_limit_bytes=60 << 20),
         name="pack_first",
-    )(factors.transpose(0, 2, 3, 1, 4), jnp.asarray(np.eye(200, 256), jnp.bfloat16), x)
+    )(
+        factors.transpose(0, 2, 3, 1, 4),
+        jnp.asarray(np.eye(200, 256), jnp.bfloat16),
+        jnp.asarray(fold_lanes(), jnp.bfloat16),
+        x,
+    )
 
 
 def pack_second_kernel(re_ref, im_ref, out_ref, order):
     fill_pack_order(order)
-    pack_rows([re_ref, im_ref], order, out_ref)
+    pack_rows([re_ref, im_ref], order, out_ref, 0)
 
 
 def pack_second(x):
     return pl.pallas_call(
         pack_second_kernel,
-        out_shape=jax.ShapeDtypeStruct((BLOCKS, ROWS, PART), jnp.bfloat16),
+        out_shape=jax.ShapeDtypeStruct((BLOCKS, XROWS, PART), jnp.bfloat16),
         grid=(1,),
         in_specs=[
             pl.BlockSpec((DEG, OWN * BLOCKS, HALF), lambda i: (0, 0, 1)),
             pl.BlockSpec((DEG, OWN * BLOCKS, HALF), lambda i: (0, 0, 3)),
         ],
-        out_specs=pl.BlockSpec((BLOCKS, ROWS, PART), lambda i: (0, 0, 0)),
+        out_specs=pl.BlockSpec((BLOCKS, XROWS, PART), lambda i: (0, 0, 0)),
         scratch_shapes=[pltpu.VMEM((4, 416, 640), jnp.bfloat16)],
         compiler_params=pltpu.CompilerParams(vmem_limit_bytes=60 << 20),
         name="pack_second",
@@ -154,15 +194,18 @@
     return 2 * group + j // 2 + step * (j % 2)
 
 
-def section_kernel(rf_ref, e_ref, mask_ref, first_ref, near_ref, far_ref, fc):
+def section_kernel(rf_ref, e_ref, mask_ref, first_ref, lanes_ref, rows_ref, near_ref, far_ref, fc):
     zeros_f = jnp.zeros((16, 256), jnp.bfloat16)
-
-    def load(b, carry):
+    rest = []
+    for b in range(BLOCKS):
         fc[b, pl.ds(96, 16), :] = zeros_f
-        fc[b, pl.ds(0, ROWS), :] = rf_ref[b]
-        return carry
-
-    lax.fori_loop(0, BLOCKS, load, 0)
+        fc[b, pl.ds(0, FROWS), :] = rf_ref[b]
+        tall = jnp.dot(rows_ref[...], rf_ref[b, :, 128:], preferred_element_type=jnp.float32)
+        rest.append(jnp.concatenate([tall[24 * q:24 * (q + 1)] for q in range(4)], axis=1))
+    rest = jnp.concatenate(rest, axis=0).astype(jnp.bfloat16)
+    rest = jnp.dot(rest, lanes_ref[...], preferred_element_type=jnp.float32)
+    for b in range(BLOCKS):
+        fc[b, pl.ds(FROWS, 24), :] = rest[24 * b:24 * (b + 1)].astype(jnp.bfloat16)
     lane_high = lax.broadcasted_iota(jnp.int32, (8, PAIR), 1) // PADR
     mask = mask_ref[...]
     for s in range(SECTIONS):
@@ -192,10 +235,12 @@
         ],
         grid=(1,),
         in_specs=[
-            pl.BlockSpec((BLOCKS, ROWS, 256), lambda i: (0, 0, 0)),
+            pl.BlockSpec((BLOCKS, FROWS, 256), lambda i: (0, 0, 0)),
             pl.BlockSpec((SECTIONS, 2, 256, PAIR), lambda i: (0, 0, 0, 0)),
             pl.BlockSpec((PADR, PAIR), lambda i: (0, 0)),
             pl.BlockSpec((8, PAIR), lambda i: (0, 0)),
+            pl.BlockSpec((512, 256), lambda i: (0, 0)),
+            pl.BlockSpec((96, FROWS), lambda i: (0, 0)),
         ],
         out_specs=[
             pl.BlockSpec((4, 12, PAIR, PAIR), lambda i: (0, 0, 0, 0)),
@@ -204,14 +249,17 @@
         scratch_shapes=[pltpu.VMEM((BLOCKS, PADR, 256), jnp.bfloat16)],
         compiler_params=pltpu.CompilerParams(vmem_limit_bytes=58 << 20),
         name="section_factors",
-    )(rf, select_matrices(), diagonal_mask(), first)
-
-
-def butterfly_kernel(half, lane_block, rx_ref, near_ref, far_ref, order_ref, *refs):
+    )(
+        rf, select_matrices(), diagonal_mask(), first,
+        jnp.asarray(fold_lanes().T, jnp.bfloat16), jnp.asarray(fold_rows().T, jnp.bfloat16),
+    )
+
+
+def butterfly_kernel(half, first_row, rx_ref, near_ref, far_ref, order_ref, *refs):
     out_ref, rs, ns, fs, stage, xa, xb, xc, xd, rsem, nsem, fsem, osem = refs[-13:]
 
     def load_rows(g):
-        rows = rx_ref.at[pl.ds(8 * g, 8), :, pl.ds(PART * lane_block, PART)]
+        rows = rx_ref.at[pl.ds(8 * g, 8), pl.ds(first_row, XROWS), :]
         return pltpu.make_async_copy(rows, rs.at[pl.ds(8 * g, 8)], rsem.at[g])
 
     def load_near(g, s):
@@ -237,7 +285,7 @@
         for q in range(2):
             load_rows(2 * i + q).wait()
             for b in range(8):
-                xa[8 * q + b, pl.ds(0, ROWS), :] = rs[16 * i + 8 * q + b]
+                xa[8 * q + b, pl.ds(0, XROWS), :] = rs[16 * i + 8 * q + b]
         src, dst = xa, xb
         for s in range(3):
             base = 16 * i if s == 2 else 0
@@ -289,16 +337,16 @@
         store(t).wait()
 
 
-def butterfly(rx, lane_block, near, far, rows):
+def butterfly(rx, first_row, near, far, rows):
     half = 0 if rows is None else 1
     anywhere = pl.BlockSpec(memory_space=pl.ANY)
     return pl.pallas_call(
-        functools.partial(butterfly_kernel, half, lane_block),
+        functools.partial(butterfly_kernel, half, first_row),
         out_shape=jax.ShapeDtypeStruct((4, 8, BANDS, SLOT, 2 * HALF), jnp.bfloat16),
         in_specs=[anywhere, anywhere, anywhere, pl.BlockSpec(memory_space=pltpu.VMEM)] + [anywhere] * half,
         out_specs=anywhere,
         scratch_shapes=[
-            pltpu.VMEM((BLOCKS, ROWS, PART), jnp.bfloat16),
+            pltpu.VMEM((BLOCKS, XROWS, PART), jnp.bfloat16),
             pltpu.VMEM((4, 12, PAIR, PAIR), jnp.bfloat16),
             pltpu.VMEM((4, 8, PAIR, PAIR), jnp.bfloat16),
             pltpu.VMEM((4, 8, BANDS, SLOT, HALF), jnp.bfloat16),
@@ -425,7 +473,7 @@
     first = jnp.pad(first, (0, PADR - ROWS))
     first = jnp.broadcast_to(jnp.concatenate([first, first])[None, :], (8, PAIR))
     near, far = section_factors(rx0, first)
-    rows = butterfly(rx0, 1, near, far, None)
+    rows = butterfly(rx0, FROWS, near, far, None)
     rows, rx1 = lax.optimization_barrier((rows, rx1))
     rows = butterfly(rx1, 0, near, far, rows).reshape(BLOCKS * BANDS, SLOT, 2 * HALF)
     u = lax.all_to_all(rows, ("wave", "lev"), 0, 0, tiled=True)

time: 168 us -> 165 us (0.982)
  waiting for transfers between devices: 66.3 us -> 61.9 us
  Pallas kernels: 51.9 us -> 54.5 us
    all_to_all x1, waiting for transfers between devices: 38.2 us -> 34 us  [body(): lax.all_to_all(pack_first(factors, coefficients), 'wave', 0, 0, tiled=True)]
    pallas_call x1, Pallas kernels: 6.74 us -> 9.19 us  [pack_first(): pl.pallas_call(pack_first_kernel, out_shape=jax.ShapeDtypeStruct((BLOCKS,...]
where the time goes in v5:
time: 165 us
  waiting for transfers between devices  61.9 us (38%)
  Pallas kernels  54.5 us (33%)
  other arithmetic  25.2 us (15%)
  starting transfers between devices  21.3 us (13%)
    all_to_all x1, waiting for transfers between devices, body(): lax.all_to_all(pack_first(factors, coefficients), 'wave', 0, 0, tiled=True)  34 us
    all_to_all x1, waiting for transfers between devices, body(): u = lax.all_to_all(rows, ('wave', 'lev'), 0, 0, tiled=True)  25 us
    pallas_call x2, Pallas kernels, butterfly(): pl.pallas_call(functools.partial(butterfly_kernel, half, first_row), out_...  19.7 us
    another operation x1, other arithmetic  16.5 us
    pallas_call x1, Pallas kernels, fourier(): pl.pallas_call(fourier_kernel, out_shape=jax.ShapeDtypeStruct((5, PART, N...  14 us
    pallas_call x1, Pallas kernels, pack_first(): pl.pallas_call(pack_first_kernel, out_shape=jax.ShapeDtypeStruct((BLOCKS,...  9.19 us
    all_to_all x1, starting transfers between devices, body(): lax.all_to_all(pack_first(factors, coefficients), 'wave', 0, 0, tiled=True)  8.6 us
    all_to_all x1, starting transfers between devices, body(): u = lax.all_to_all(rows, ('wave', 'lev'), 0, 0, tiled=True)  7.86 us
  transfers between devices with their start and end apart: 3, of which 3 were waited for; matrix products, arithmetic and copies ran while one was open for 16% of the time, Pallas kernels for 13%

profile of v5, /device:TPU:1, one launch (start us, length us, event | category | flops | bytes accessed | tf_op | source)
XLA Modules:
  0.0 164.5 jit_solution(7172679608522377415)
XLA Ops:
  0.0 9.2 %pack_first.1 = bf16[32,184,256]{2,1,0:T(8,128)(2,1)} custom-call(bf16[5,20,20,2,160]{4,3,2,1,0:T(2,128)(2,1)} %bitcast.4, bf16[200,256]{1,0:T(8,128)(2,1)} %constant.190.clone.eye_ref, bf16[256,512]{1,0:T(8,128)(2,1)} %constant.191.clone.lanes_ref, bf16[20,160,512]{2,1,0:T(8,128)(2,1)} %x_ref.1), custom_call_target="tpu_custom_call" | custom-call | tf_op jit(solution)/shard_map/pack_first/pallas_call | solution.py:138
  9.2 8.6 %all-to-all-start = ((bf16[32,184,256]{2,1,0:T(8,128)(2,1)}), bf16[32,184,256]{2,1,0:T(8,128)(2,1)S(1)}, u32[]{:S(2)}, u32[]{:S(2)}) async-start(bf16[32,184,256]{2,1,0:T(8,128)(2,1)} %pack_first.1), calls=%async_computation | async-start | bytes 6029312 | tf_op jit(solution)/shard_map/all_to_all | solution.py:468
  17.8 0.0 copy-start.1
  17.8 4.2 %pack_second.1 = bf16[32,104,256]{2,1,0:T(8,128)(2,1)} custom-call(bf16[20,160,512]{2,1,0:T(8,128)(2,1)} %x_ref.1, bf16[20,160,512]{2,1,0:T(8,128)(2,1)} %x_ref.1), custom_call_target="tpu_custom_call" | custom-call | tf_op jit(solution)/shard_map/pack_second/pallas_call | solution.py:167
  22.0 0.0 copy-done.1
  22.0 0.1 dynamic_slice.3
  22.1 0.1 iota_subtract_fusion
  22.2 34.0 %all-to-all-done.rf_ref.rx_ref = bf16[32,184,256]{2,1,0:T(8,128)(2,1)S(1)} async-done(((bf16[32,184,256]{2,1,0:T(8,128)(2,1)}), bf16[32,184,256]{2,1,0:T(8,128)(2,1)S(1)}, u32[]{:S(2)}, u32[]{:S(2)}) %all-to-all-start) | async-done | bytes 3014688 | tf_op jit(solution)/shard_map/all_to_all | solution.py:468
  56.2 0.0 copy-start
  56.2 4.8 %all-to-all-start.1 = ((bf16[32,104,256]{2,1,0:T(8,128)(2,1)}), bf16[32,104,256]{2,1,0:T(8,128)(2,1)}, u32[]{:S(2)}, u32[]{:S(2)}) async-start(bf16[32,104,256]{2,1,0:T(8,128)(2,1)} %pack_second.1), calls=%async_computation.1 | async-start | bytes 3407872 | tf_op jit(solution)/shard_map/all_to_all | solution.py:470
  61.0 0.1 sub.84
  61.1 0.1 pad_add_fusion
  61.3 0.8 fusion.54.mask_ref
  62.0 1.0 fusion.46.order_ref
  63.1 1.3 fusion.13.e_ref
  64.4 0.6 broadcast_in_dim.8.first_ref
  65.0 0.0 copy-done
  65.0 7.4 %section_factors.1 = (bf16[4,12,224,224]{3,2,1,0:T(8,128)(2,1)}, bf16[4,8,224,224]{3,2,1,0:T(8,128)(2,1)}) custom-call(bf16[32,184,256]{2,1,0:T(8,128)(2,1)} %copy-done, bf16[5,2,256,224]{3,2,1,0:T(8,128)(2,1)} %fusion.13.e_ref, f32[112,224]{1,0:T(8,128)} %fusion.54.mask_ref, s32[8,224]{1,0:T(8,128)} %broadcast_in_dim.8.first_ref, ...), custom_call_target="tpu_custom_call" | custom-call | tf_op jit(solution)/shard_map/section_factors/pallas_call | solution.py:230
  72.4 9.8 %butterfly.2.refs_0_ = bf16[4,8,4,56,256]{4,3,2,1,0:T(8,128)(2,1)} custom-call(bf16[32,184,256]{2,1,0:T(8,128)(2,1)} %copy-done, bf16[4,12,224,224]{3,2,1,0:T(8,128)(2,1)} %get-tuple-element.12.near_ref, bf16[4,8,224,224]{3,2,1,0:T(8,128)(2,1)} %get-tuple-element.13.far_ref, bf16[224,224]{1,0:T(8,128)(2,1)} %fusion.46.order_ref), custom_call_target="tpu_custom_call" | custom-call | tf_op jit(solution)/shard_map/butterfly/pallas_call | solution.py:343
  82.3 3.0 %all-to-all-done.1.rx_ref = bf16[32,104,256]{2,1,0:T(8,128)(2,1)} async-done(((bf16[32,104,256]{2,1,0:T(8,128)(2,1)}), bf16[32,104,256]{2,1,0:T(8,128)(2,1)}, u32[]{:S(2)}, u32[]{:S(2)}) %all-to-all-start.1) | async-done | bytes 1703968 | tf_op jit(solution)/shard_map/all_to_all | solution.py:470
  85.2 9.8 %butterfly.3 = bf16[4,8,4,56,256]{4,3,2,1,0:T(8,128)(2,1)} custom-call(bf16[32,104,256]{2,1,0:T(8,128)(2,1)} %all-to-all-done.1.rx_ref, bf16[4,12,224,224]{3,2,1,0:T(8,128)(2,1)} %get-tuple-element.12.near_ref, bf16[4,8,224,224]{3,2,1,0:T(8,128)(2,1)} %get-tuple-element.13.far_ref, ...), custom_call_target="tpu_custom_call", output_to_operand_aliasing={{}: (4, {})} | custom-call | tf_op jit(solution)/shard_map/butterfly/pallas_call | solution.py:343
  95.1 7.9 %all-to-all-start.2 = ((bf16[128,56,256]{2,1,0:T(8,128)(2,1)}), bf16[128,56,256]{2,1,0:T(8,128)(2,1)}, u32[]{:S(2)}, u32[]{:S(2)}) async-start(bf16[128,56,256]{2,1,0:T(8,128)(2,1)} %bitcast.3), calls=%async_computation.2 | async-start | bytes 7340032 | tf_op jit(solution)/shard_map/all_to_all | solution.py:479
  103.0 0.2 reshape.29
  103.2 0.2 reshape.30
  103.5 0.7 fusion.30.mirror_ref
  104.2 2.5 %fusion.24.order_ref = bf16[400,448]{1,0:T(8,128)(2,1)} fusion(s32[400]{0:T(512)S(1)} %get-tuple-element.37, s32[400]{0:T(512)S(1)} %get-tuple-element.47, s32[400]{0:T(512)S(1)} %get-tuple-element.38, s32[400]{0:T(512)S(1)} %get-tuple-element.42, s32[400]{0:T(512)S(1)} %get-tuple-element.39, s32[400]{0:T(512)S(1)} %get-tuple-element.48, ...), kind=kLoop, calls=%fused_computation.38 | loop fusion | flops 4659200 | bytes 372800 | tf_op jit(solution)/shard_map/convert_element_type | solution.py:187
  106.7 16.5 %multiply_convert_fusion.1 = (bf16[640,1408]{1,0:T(8,128)(2,1)S(1)}, bf16[640,1408]{1,0:T(8,128)(2,1)S(1)}) fusion(s32[640]{0:T(1024)S(1)} %reshape.30, f32[640]{0:T(1024)S(1)} %get-tuple-element.19, f32[640]{0:T(1024)S(1)} %get-tuple-element.20), kind=kLoop, calls=%fused_computation.10 | loop fusion | flops 11714560 | bytes 3612160 | tf_op jit(solution)/shard_map/convert
  123.2 2.2 %pad_maximum_fusion.table_ref.middle_ref = bf16[1280,1408]{1,0:T(8,128)(2,1)} fusion(bf16[640,1408]{1,0:T(8,128)(2,1)S(1)} %get-tuple-element.18, bf16[640,1408]{1,0:T(8,128)(2,1)S(1)} %get-tuple-element.17), kind=kLoop, calls=%fused_computation.8 | loop fusion | flops 7208960 | bytes 7208960 | tf_op jit(solution)/shard_map/concatenate | solution.py:462
  125.4 25.0 %all-to-all-done.2.u_ref = bf16[128,56,256]{2,1,0:T(8,128)(2,1)} async-done(((bf16[128,56,256]{2,1,0:T(8,128)(2,1)}), bf16[128,56,256]{2,1,0:T(8,128)(2,1)}, u32[]{:S(2)}, u32[]{:S(2)}) %all-to-all-start.2) | async-done | bytes 3670048 | tf_op jit(solution)/shard_map/all_to_all | solution.py:479
  150.3 14.0 %fourier.1 = bf16[5,256,2560]{2,1,0:T(8,128)(2,1)} custom-call(bf16[128,56,256]{2,1,0:T(8,128)(2,1)} %all-to-all-done.2.u_ref, bf16[400,448]{1,0:T(8,128)(2,1)} %fusion.24.order_ref, bf16[256,256]{1,0:T(8,128)(2,1)} %fusion.30.mirror_ref, bf16[1280,1408]{1,0:T(8,128)(2,1)} %pad_maximum_fusion.table_ref.middle_ref, ...), custom_call_target="tpu_custom_call" | custom-call | tf_op jit(solution)/shard_map/fourier/pallas_call | solution.py:431
  (18 shorter events, 0.2 us)
Async XLA Ops:
  9.2 47.0 %all-to-all-start = ((bf16[32,184,256]{2,1,0:T(8,128)(2,1)}), bf16[32,184,256]{2,1,0:T(8,128)(2,1)S(1)}, u32[]{:S(2)}, u32[]{:S(2)}) async-start(bf16[32,184,256]{2,1,0:T(8,128)(2,1)} %pack_first.1), calls=%async_computation | async-start | bytes 6029312 | tf_op jit(solution)/shard_map/all_to_all | solution.py:468
  17.8 4.2 %copy-start.1 = (s32[640]{0:T(1024)S(1)}, s32[640]{0:T(1024)}, u32[]{:S(2)}) copy-start(s32[640]{0:T(1024)} %param.9) | copy-start | bytes 7684
  56.2 8.8 %copy-start = (bf16[32,184,256]{2,1,0:T(8,128)(2,1)}, bf16[32,184,256]{2,1,0:T(8,128)(2,1)S(1)}, u32[]{:S(2)}) copy-start(bf16[32,184,256]{2,1,0:T(8,128)(2,1)S(1)} %all-to-all-done.rf_ref.rx_ref) | copy-start | bytes 9043972
  56.2 29.1 %all-to-all-start.1 = ((bf16[32,104,256]{2,1,0:T(8,128)(2,1)}), bf16[32,104,256]{2,1,0:T(8,128)(2,1)}, u32[]{:S(2)}, u32[]{:S(2)}) async-start(bf16[32,104,256]{2,1,0:T(8,128)(2,1)} %pack_second.1), calls=%async_computation.1 | async-start | bytes 3407872 | tf_op jit(solution)/shard_map/all_to_all | solution.py:470
  95.1 55.2 %all-to-all-start.2 = ((bf16[128,56,256]{2,1,0:T(8,128)(2,1)}), bf16[128,56,256]{2,1,0:T(8,128)(2,1)}, u32[]{:S(2)}, u32[]{:S(2)}) async-start(bf16[128,56,256]{2,1,0:T(8,128)(2,1)} %bitcast.3), calls=%async_computation.2 | async-start | bytes 7340032 | tf_op jit(solution)/shard_map/all_to_all | solution.py:479

commit v6 on v5

--- a/solution.py
+++ b/solution.py
@@ -52,15 +52,15 @@
 
 
 def fill_pack_order(order):
-    shape = (4 * 104, DEG * 32)
+    shape = (4 * 104, DEG * 24)
     row = lax.broadcasted_iota(jnp.int32, shape, 0)
     col = lax.broadcasted_iota(jnp.int32, shape, 1)
     owner = (row >= 104).astype(jnp.int32) + (row >= 208).astype(jnp.int32) + (row >= 312).astype(jnp.int32)
     inner = row - 104 * owner
     k = sum((inner >= DEG * i).astype(jnp.int32) for i in range(1, OWN))
-    base = (inner - DEG * k) * 32 + OWN * owner + k
+    base = (inner - DEG * k) * 24 + OWN * owner + k
     ahead = jnp.where(inner < ROWS, col - base, -1)
-    for v in range(4):
+    for v in range(2):
         order[v] = (ahead == 4 * v).astype(jnp.float32).astype(jnp.bfloat16)
 
 
@@ -83,8 +83,9 @@
 
 def chosen_rows(srcs, order, group):
     start = 4 * OWN * group
-    at = start // 16 * 16
-    window = jnp.concatenate([src[:, at:at + 32, :].reshape(DEG * 32, src.shape[2]) for src in srcs], axis=1)
+    at = start // 8 * 8
+    window = jnp.concatenate([src[:, at:at + 24, :].reshape(DEG * 24, src.shape[2]) for src in srcs], axis=1)
+    window = window.astype(jnp.bfloat16)
     return jnp.dot(order[(start - at) // 4], window, preferred_element_type=jnp.float32)
 
 
@@ -120,14 +121,16 @@
     for o in range(DEG):
         left = jnp.concatenate([f_ref[s, o].reshape(2 * DEG, OWN * BLOCKS) for s in range(SECTIONS)], axis=0)
         y = lax.dot_general(left, eye_ref[...], (((0,), (0,)), ((), ())), preferred_element_type=jnp.float32)
-        turned[o] = y.astype(jnp.bfloat16)
+        turned[o] = y
     pack_folded(turned, order, lanes_ref, stage)
     pieces = [pl.ds(0, FROWS), pl.ds(FROWS, XROWS)]
     store = [pltpu.make_async_copy(stage.at[:, at, :], out_ref.at[:, at, :], osem.at[i]) for i, at in enumerate(pieces)]
     store[0].start()
     for copy in fetch:
         copy.wait()
-    pack_rows([xs], order, stage, FROWS)
+    for n in range(DEG):
+        turned[n] = xs[n].astype(jnp.float32)
+    pack_rows([turned], order, stage, FROWS)
     store[1].start()
     for copy in store:
         copy.wait()
@@ -141,8 +144,8 @@
         in_specs=[here, here, here, pl.BlockSpec(memory_space=pl.ANY)],
         out_specs=pl.BlockSpec(memory_space=pl.ANY),
         scratch_shapes=[
-            pltpu.VMEM((DEG, OWN * BLOCKS, 256), jnp.bfloat16),
-            pltpu.VMEM((4, 416, 640), jnp.bfloat16),
+            pltpu.VMEM((DEG, OWN * BLOCKS, 256), jnp.float32),
+            pltpu.VMEM((2, 416, 480), jnp.bfloat16),
             pltpu.VMEM((DEG, OWN * BLOCKS, PART), jnp.bfloat16),
             pltpu.VMEM((BLOCKS, FROWS + XROWS, PART), jnp.bfloat16),
             pltpu.SemaphoreType.DMA((2,)),
@@ -158,9 +161,12 @@
     )
 
 
-def pack_second_kernel(re_ref, im_ref, out_ref, order):
+def pack_second_kernel(re_ref, im_ref, out_ref, order, wide):
     fill_pack_order(order)
-    pack_rows([re_ref, im_ref], order, out_ref, 0)
+    for n in range(DEG):
+        wide[n, :, pl.ds(0, HALF)] = re_ref[n].astype(jnp.float32)
+        wide[n, :, pl.ds(HALF, HALF)] = im_ref[n].astype(jnp.float32)
+    pack_rows([wide], order, out_ref, 0)
 
 
 def pack_second(x):
@@ -173,7 +179,7 @@
             pl.BlockSpec((DEG, OWN * BLOCKS, HALF), lambda i: (0, 0, 3)),
         ],
         out_specs=pl.BlockSpec((BLOCKS, XROWS, PART), lambda i: (0, 0, 0)),
-        scratch_shapes=[pltpu.VMEM((4, 416, 640), jnp.bfloat16)],
+        scratch_shapes=[pltpu.VMEM((2, 416, 480), jnp.bfloat16), pltpu.VMEM((DEG, OWN * BLOCKS, PART), jnp.float32)],
         compiler_params=pltpu.CompilerParams(vmem_limit_bytes=60 << 20),
         name="pack_second",
     )(x, x)

time: 165 us -> 164 us (level)
  Pallas kernels: 54.5 us -> 52.8 us
where the time goes in v6:
time: 164 us; the launch traced here: 163 us
  waiting for transfers between devices  62.4 us (38%)
  Pallas kernels  52.8 us (32%)
  other arithmetic  25.2 us (15%)
  starting transfers between devices  21.3 us (13%)
    all_to_all x1, waiting for transfers between devices, body(): lax.all_to_all(pack_first(factors, coefficients), 'wave', 0, 0, tiled=True)  34.4 us
    all_to_all x1, waiting for transfers between devices, body(): u = lax.all_to_all(rows, ('wave', 'lev'), 0, 0, tiled=True)  25 us
    pallas_call x2, Pallas kernels, butterfly(): pl.pallas_call(functools.partial(butterfly_kernel, half, first_row), out_...  19.7 us
    another operation x1, other arithmetic  16.5 us
    pallas_call x1, Pallas kernels, fourier(): pl.pallas_call(fourier_kernel, out_shape=jax.ShapeDtypeStruct((5, PART, N...  14 us
    all_to_all x1, starting transfers between devices, body(): lax.all_to_all(pack_first(factors, coefficients), 'wave', 0, 0, tiled=True)  8.6 us
    pallas_call x1, Pallas kernels, pack_first(): pl.pallas_call(pack_first_kernel, out_shape=jax.ShapeDtypeStruct((BLOCKS,...  7.91 us
    all_to_all x1, starting transfers between devices, body(): u = lax.all_to_all(rows, ('wave', 'lev'), 0, 0, tiled=True)  7.86 us
  transfers between devices with their start and end apart: 3, of which 3 were waited for; matrix products, arithmetic and copies ran while one was open for 16% of the time, Pallas kernels for 13%

profile of v6, /device:TPU:1, one launch (start us, length us, event | category | flops | bytes accessed | tf_op | source)
XLA Modules:
  0.0 163.3 jit_solution(6184904885412696062)
XLA Ops:
  0.0 7.9 %pack_first.1 = bf16[32,184,256]{2,1,0:T(8,128)(2,1)} custom-call(bf16[5,20,20,2,160]{4,3,2,1,0:T(2,128)(2,1)} %bitcast.4, bf16[200,256]{1,0:T(8,128)(2,1)} %constant.190.clone.eye_ref, bf16[256,512]{1,0:T(8,128)(2,1)} %constant.191.clone.lanes_ref, bf16[20,160,512]{2,1,0:T(8,128)(2,1)} %x_ref.1), custom_call_target="tpu_custom_call" | custom-call | tf_op jit(solution)/shard_map/pack_first/pallas_call | solution.py:141
  7.9 8.6 %all-to-all-start = ((bf16[32,184,256]{2,1,0:T(8,128)(2,1)}), bf16[32,184,256]{2,1,0:T(8,128)(2,1)S(1)}, u32[]{:S(2)}, u32[]{:S(2)}) async-start(bf16[32,184,256]{2,1,0:T(8,128)(2,1)} %pack_first.1), calls=%async_computation | async-start | bytes 6029312 | tf_op jit(solution)/shard_map/all_to_all | solution.py:474
  16.5 0.0 copy-start.1
  16.5 3.8 %pack_second.1 = bf16[32,104,256]{2,1,0:T(8,128)(2,1)} custom-call(bf16[20,160,512]{2,1,0:T(8,128)(2,1)} %x_ref.1, bf16[20,160,512]{2,1,0:T(8,128)(2,1)} %x_ref.1), custom_call_target="tpu_custom_call" | custom-call | tf_op jit(solution)/shard_map/pack_second/pallas_call | solution.py:173
  20.3 0.0 copy-done.1
  20.3 0.1 dynamic_slice.3
  20.4 0.1 iota_subtract_fusion
  20.5 34.4 %all-to-all-done.rf_ref.rx_ref = bf16[32,184,256]{2,1,0:T(8,128)(2,1)S(1)} async-done(((bf16[32,184,256]{2,1,0:T(8,128)(2,1)}), bf16[32,184,256]{2,1,0:T(8,128)(2,1)S(1)}, u32[]{:S(2)}, u32[]{:S(2)}) %all-to-all-start) | async-done | bytes 3014688 | tf_op jit(solution)/shard_map/all_to_all | solution.py:474
  54.9 0.0 copy-start
  54.9 4.8 %all-to-all-start.1 = ((bf16[32,104,256]{2,1,0:T(8,128)(2,1)}), bf16[32,104,256]{2,1,0:T(8,128)(2,1)}, u32[]{:S(2)}, u32[]{:S(2)}) async-start(bf16[32,104,256]{2,1,0:T(8,128)(2,1)} %pack_second.1), calls=%async_computation.1 | async-start | bytes 3407872 | tf_op jit(solution)/shard_map/all_to_all | solution.py:476
  59.8 0.1 sub.84
  59.9 0.1 pad_add_fusion
  60.0 0.8 fusion.54.mask_ref
  60.8 1.0 fusion.46.order_ref
  61.8 1.3 fusion.13.e_ref
  63.1 0.6 broadcast_in_dim.8.first_ref
  63.7 0.0 copy-done
  63.7 7.4 %section_factors.1 = (bf16[4,12,224,224]{3,2,1,0:T(8,128)(2,1)}, bf16[4,8,224,224]{3,2,1,0:T(8,128)(2,1)}) custom-call(bf16[32,184,256]{2,1,0:T(8,128)(2,1)} %copy-done, bf16[5,2,256,224]{3,2,1,0:T(8,128)(2,1)} %fusion.13.e_ref, f32[112,224]{1,0:T(8,128)} %fusion.54.mask_ref, s32[8,224]{1,0:T(8,128)} %broadcast_in_dim.8.first_ref, ...), custom_call_target="tpu_custom_call" | custom-call | tf_op jit(solution)/shard_map/section_factors/pallas_call | solution.py:236
  71.1 9.8 %butterfly.2.refs_0_ = bf16[4,8,4,56,256]{4,3,2,1,0:T(8,128)(2,1)} custom-call(bf16[32,184,256]{2,1,0:T(8,128)(2,1)} %copy-done, bf16[4,12,224,224]{3,2,1,0:T(8,128)(2,1)} %get-tuple-element.12.near_ref, bf16[4,8,224,224]{3,2,1,0:T(8,128)(2,1)} %get-tuple-element.13.far_ref, bf16[224,224]{1,0:T(8,128)(2,1)} %fusion.46.order_ref), custom_call_target="tpu_custom_call" | custom-call | tf_op jit(solution)/shard_map/butterfly/pallas_call | solution.py:349
  81.0 3.0 %all-to-all-done.1.rx_ref = bf16[32,104,256]{2,1,0:T(8,128)(2,1)} async-done(((bf16[32,104,256]{2,1,0:T(8,128)(2,1)}), bf16[32,104,256]{2,1,0:T(8,128)(2,1)}, u32[]{:S(2)}, u32[]{:S(2)}) %all-to-all-start.1) | async-done | bytes 1703968 | tf_op jit(solution)/shard_map/all_to_all | solution.py:476
  84.0 9.9 %butterfly.3 = bf16[4,8,4,56,256]{4,3,2,1,0:T(8,128)(2,1)} custom-call(bf16[32,104,256]{2,1,0:T(8,128)(2,1)} %all-to-all-done.1.rx_ref, bf16[4,12,224,224]{3,2,1,0:T(8,128)(2,1)} %get-tuple-element.12.near_ref, bf16[4,8,224,224]{3,2,1,0:T(8,128)(2,1)} %get-tuple-element.13.far_ref, ...), custom_call_target="tpu_custom_call", output_to_operand_aliasing={{}: (4, {})} | custom-call | tf_op jit(solution)/shard_map/butterfly/pallas_call | solution.py:349
  93.8 7.9 %all-to-all-start.2 = ((bf16[128,56,256]{2,1,0:T(8,128)(2,1)}), bf16[128,56,256]{2,1,0:T(8,128)(2,1)}, u32[]{:S(2)}, u32[]{:S(2)}) async-start(bf16[128,56,256]{2,1,0:T(8,128)(2,1)} %bitcast.3), calls=%async_computation.2 | async-start | bytes 7340032 | tf_op jit(solution)/shard_map/all_to_all | solution.py:485
  101.7 0.2 reshape.29
  101.9 0.2 reshape.30
  102.2 0.7 fusion.30.mirror_ref
  102.9 2.5 %fusion.24.order_ref = bf16[400,448]{1,0:T(8,128)(2,1)} fusion(s32[400]{0:T(512)S(1)} %get-tuple-element.37, s32[400]{0:T(512)S(1)} %get-tuple-element.47, s32[400]{0:T(512)S(1)} %get-tuple-element.38, s32[400]{0:T(512)S(1)} %get-tuple-element.42, s32[400]{0:T(512)S(1)} %get-tuple-element.39, s32[400]{0:T(512)S(1)} %get-tuple-element.48, ...), kind=kLoop, calls=%fused_computation.38 | loop fusion | flops 4659200 | bytes 372800 | tf_op jit(solution)/shard_map/convert_element_type | solution.py:193
  105.4 16.5 %multiply_convert_fusion.1 = (bf16[640,1408]{1,0:T(8,128)(2,1)S(1)}, bf16[640,1408]{1,0:T(8,128)(2,1)S(1)}) fusion(s32[640]{0:T(1024)S(1)} %reshape.30, f32[640]{0:T(1024)S(1)} %get-tuple-element.19, f32[640]{0:T(1024)S(1)} %get-tuple-element.20), kind=kLoop, calls=%fused_computation.10 | loop fusion | flops 11714560 | bytes 3612160 | tf_op jit(solution)/shard_map/convert
  121.9 2.2 %pad_maximum_fusion.table_ref.middle_ref = bf16[1280,1408]{1,0:T(8,128)(2,1)} fusion(bf16[640,1408]{1,0:T(8,128)(2,1)S(1)} %get-tuple-element.18, bf16[640,1408]{1,0:T(8,128)(2,1)S(1)} %get-tuple-element.17), kind=kLoop, calls=%fused_computation.8 | loop fusion | flops 7208960 | bytes 7208960 | tf_op jit(solution)/shard_map/concatenate | solution.py:468
  124.1 25.0 %all-to-all-done.2.u_ref = bf16[128,56,256]{2,1,0:T(8,128)(2,1)} async-done(((bf16[128,56,256]{2,1,0:T(8,128)(2,1)}), bf16[128,56,256]{2,1,0:T(8,128)(2,1)}, u32[]{:S(2)}, u32[]{:S(2)}) %all-to-all-start.2) | async-done | bytes 3670048 | tf_op jit(solution)/shard_map/all_to_all | solution.py:485
  149.1 14.0 %fourier.1 = bf16[5,256,2560]{2,1,0:T(8,128)(2,1)} custom-call(bf16[128,56,256]{2,1,0:T(8,128)(2,1)} %all-to-all-done.2.u_ref, bf16[400,448]{1,0:T(8,128)(2,1)} %fusion.24.order_ref, bf16[256,256]{1,0:T(8,128)(2,1)} %fusion.30.mirror_ref, bf16[1280,1408]{1,0:T(8,128)(2,1)} %pad_maximum_fusion.table_ref.middle_ref, ...), custom_call_target="tpu_custom_call" | custom-call | tf_op jit(solution)/shard_map/fourier/pallas_call | solution.py:437
  (18 shorter events, 0.2 us)
Async XLA Ops:
  7.9 47.0 %all-to-all-start = ((bf16[32,184,256]{2,1,0:T(8,128)(2,1)}), bf16[32,184,256]{2,1,0:T(8,128)(2,1)S(1)}, u32[]{:S(2)}, u32[]{:S(2)}) async-start(bf16[32,184,256]{2,1,0:T(8,128)(2,1)} %pack_first.1), calls=%async_computation | async-start | bytes 6029312 | tf_op jit(solution)/shard_map/all_to_all | solution.py:474
  16.5 3.8 %copy-start.1 = (s32[640]{0:T(1024)S(1)}, s32[640]{0:T(1024)}, u32[]{:S(2)}) copy-start(s32[640]{0:T(1024)} %param.9) | copy-start | bytes 7684
  54.9 8.8 %copy-start = (bf16[32,184,256]{2,1,0:T(8,128)(2,1)}, bf16[32,184,256]{2,1,0:T(8,128)(2,1)S(1)}, u32[]{:S(2)}) copy-start(bf16[32,184,256]{2,1,0:T(8,128)(2,1)S(1)} %all-to-all-done.rf_ref.rx_ref) | copy-start | bytes 9043972
  54.9 29.1 %all-to-all-start.1 = ((bf16[32,104,256]{2,1,0:T(8,128)(2,1)}), bf16[32,104,256]{2,1,0:T(8,128)(2,1)}, u32[]{:S(2)}, u32[]{:S(2)}) async-start(bf16[32,104,256]{2,1,0:T(8,128)(2,1)} %pack_second.1), calls=%async_computation.1 | async-start | bytes 3407872 | tf_op jit(solution)/shard_map/all_to_all | solution.py:476
  93.8 55.2 %all-to-all-start.2 = ((bf16[128,56,256]{2,1,0:T(8,128)(2,1)}), bf16[128,56,256]{2,1,0:T(8,128)(2,1)}, u32[]{:S(2)}, u32[]{:S(2)}) async-start(bf16[128,56,256]{2,1,0:T(8,128)(2,1)} %bitcast.3), calls=%async_computation.2 | async-start | bytes 7340032 | tf_op jit(solution)/shard_map/all_to_all | solution.py:485

commit v7 on v6

--- a/solution.py
+++ b/solution.py
@@ -310,7 +310,7 @@
             src, dst = dst, src
         return carry
 
-    lax.fori_loop(0, 2, early, 0)
+    lax.fori_loop(0, 2, early, 0, unroll=True)
 
     def late(i, carry):
         for q in range(2):
@@ -338,7 +338,7 @@
             store(2 * i + q).start()
         return carry
 
-    lax.fori_loop(0, 2, late, 0)
+    lax.fori_loop(0, 2, late, 0, unroll=True)
     for t in range(4):
         store(t).wait()
 

time: 164 us -> 164 us (level)
  no operation moved by 1% of the time
where the time goes in v7:
time: 164 us; the launch traced here: 163 us
  waiting for transfers between devices  62.4 us (38%)
  Pallas kernels  52.8 us (32%)
  other arithmetic  25.2 us (15%)
  starting transfers between devices  21.3 us (13%)
    all_to_all x1, waiting for transfers between devices, body(): lax.all_to_all(pack_first(factors, coefficients), 'wave', 0, 0, tiled=True)  34.4 us
    all_to_all x1, waiting for transfers between devices, body(): u = lax.all_to_all(rows, ('wave', 'lev'), 0, 0, tiled=True)  25 us
    pallas_call x2, Pallas kernels, butterfly(): pl.pallas_call(functools.partial(butterfly_kernel, half, first_row), out_...  19.7 us
    another operation x1, other arithmetic  16.5 us
    pallas_call x1, Pallas kernels, fourier(): pl.pallas_call(fourier_kernel, out_shape=jax.ShapeDtypeStruct((5, PART, N...  14 us
    all_to_all x1, starting transfers between devices, body(): lax.all_to_all(pack_first(factors, coefficients), 'wave', 0, 0, tiled=True)  8.6 us
    pallas_call x1, Pallas kernels, pack_first(): pl.pallas_call(pack_first_kernel, out_shape=jax.ShapeDtypeStruct((BLOCKS,...  7.91 us
    all_to_all x1, starting transfers between devices, body(): u = lax.all_to_all(rows, ('wave', 'lev'), 0, 0, tiled=True)  7.89 us
  transfers between devices with their start and end apart: 3, of which 3 were waited for; matrix products, arithmetic and copies ran while one was open for 16% of the time, Pallas kernels for 13%

profile of v7, /device:TPU:1, one launch (start us, length us, event | category | flops | bytes accessed | tf_op | source)
XLA Modules:
  0.0 163.3 jit_solution(10977825890611007202)
XLA Ops:
  0.0 7.9 %pack_first.1 = bf16[32,184,256]{2,1,0:T(8,128)(2,1)} custom-call(bf16[5,20,20,2,160]{4,3,2,1,0:T(2,128)(2,1)} %bitcast.4, bf16[200,256]{1,0:T(8,128)(2,1)} %constant.190.clone.eye_ref, bf16[256,512]{1,0:T(8,128)(2,1)} %constant.191.clone.lanes_ref, bf16[20,160,512]{2,1,0:T(8,128)(2,1)} %x_ref.1), custom_call_target="tpu_custom_call" | custom-call | tf_op jit(solution)/shard_map/pack_first/pallas_call | solution.py:141
  7.9 8.6 %all-to-all-start = ((bf16[32,184,256]{2,1,0:T(8,128)(2,1)}), bf16[32,184,256]{2,1,0:T(8,128)(2,1)S(1)}, u32[]{:S(2)}, u32[]{:S(2)}) async-start(bf16[32,184,256]{2,1,0:T(8,128)(2,1)} %pack_first.1), calls=%async_computation | async-start | bytes 6029312 | tf_op jit(solution)/shard_map/all_to_all | solution.py:474
  16.5 0.0 copy-start.1
  16.5 3.8 %pack_second.1 = bf16[32,104,256]{2,1,0:T(8,128)(2,1)} custom-call(bf16[20,160,512]{2,1,0:T(8,128)(2,1)} %x_ref.1, bf16[20,160,512]{2,1,0:T(8,128)(2,1)} %x_ref.1), custom_call_target="tpu_custom_call" | custom-call | tf_op jit(solution)/shard_map/pack_second/pallas_call | solution.py:173
  20.3 0.0 copy-done.1
  20.3 0.1 dynamic_slice.3
  20.4 0.1 iota_subtract_fusion
  20.5 34.4 %all-to-all-done.rf_ref.rx_ref = bf16[32,184,256]{2,1,0:T(8,128)(2,1)S(1)} async-done(((bf16[32,184,256]{2,1,0:T(8,128)(2,1)}), bf16[32,184,256]{2,1,0:T(8,128)(2,1)S(1)}, u32[]{:S(2)}, u32[]{:S(2)}) %all-to-all-start) | async-done | bytes 3014688 | tf_op jit(solution)/shard_map/all_to_all | solution.py:474
  54.9 0.0 copy-start
  54.9 4.8 %all-to-all-start.1 = ((bf16[32,104,256]{2,1,0:T(8,128)(2,1)}), bf16[32,104,256]{2,1,0:T(8,128)(2,1)}, u32[]{:S(2)}, u32[]{:S(2)}) async-start(bf16[32,104,256]{2,1,0:T(8,128)(2,1)} %pack_second.1), calls=%async_computation.1 | async-start | bytes 3407872 | tf_op jit(solution)/shard_map/all_to_all | solution.py:476
  59.8 0.1 sub.84
  59.9 0.1 pad_add_fusion
  60.0 0.8 fusion.54.mask_ref
  60.8 1.0 fusion.46.order_ref
  61.8 1.3 fusion.13.e_ref
  63.1 0.6 broadcast_in_dim.8.first_ref
  63.7 0.0 copy-done
  63.7 7.4 %section_factors.1 = (bf16[4,12,224,224]{3,2,1,0:T(8,128)(2,1)}, bf16[4,8,224,224]{3,2,1,0:T(8,128)(2,1)}) custom-call(bf16[32,184,256]{2,1,0:T(8,128)(2,1)} %copy-done, bf16[5,2,256,224]{3,2,1,0:T(8,128)(2,1)} %fusion.13.e_ref, f32[112,224]{1,0:T(8,128)} %fusion.54.mask_ref, s32[8,224]{1,0:T(8,128)} %broadcast_in_dim.8.first_ref, ...), custom_call_target="tpu_custom_call" | custom-call | tf_op jit(solution)/shard_map/section_factors/pallas_call | solution.py:236
  71.1 9.8 %butterfly.2.refs_0_ = bf16[4,8,4,56,256]{4,3,2,1,0:T(8,128)(2,1)} custom-call(bf16[32,184,256]{2,1,0:T(8,128)(2,1)} %copy-done, bf16[4,12,224,224]{3,2,1,0:T(8,128)(2,1)} %get-tuple-element.12.near_ref, bf16[4,8,224,224]{3,2,1,0:T(8,128)(2,1)} %get-tuple-element.13.far_ref, bf16[224,224]{1,0:T(8,128)(2,1)} %fusion.46.order_ref), custom_call_target="tpu_custom_call" | custom-call | tf_op jit(solution)/shard_map/butterfly/pallas_call | solution.py:349
  81.0 3.0 %all-to-all-done.1.rx_ref = bf16[32,104,256]{2,1,0:T(8,128)(2,1)} async-done(((bf16[32,104,256]{2,1,0:T(8,128)(2,1)}), bf16[32,104,256]{2,1,0:T(8,128)(2,1)}, u32[]{:S(2)}, u32[]{:S(2)}) %all-to-all-start.1) | async-done | bytes 1703968 | tf_op jit(solution)/shard_map/all_to_all | solution.py:476
  84.0 9.8 %butterfly.3 = bf16[4,8,4,56,256]{4,3,2,1,0:T(8,128)(2,1)} custom-call(bf16[32,104,256]{2,1,0:T(8,128)(2,1)} %all-to-all-done.1.rx_ref, bf16[4,12,224,224]{3,2,1,0:T(8,128)(2,1)} %get-tuple-element.12.near_ref, bf16[4,8,224,224]{3,2,1,0:T(8,128)(2,1)} %get-tuple-element.13.far_ref, ...), custom_call_target="tpu_custom_call", output_to_operand_aliasing={{}: (4, {})} | custom-call | tf_op jit(solution)/shard_map/butterfly/pallas_call | solution.py:349
  93.8 7.9 %all-to-all-start.2 = ((bf16[128,56,256]{2,1,0:T(8,128)(2,1)}), bf16[128,56,256]{2,1,0:T(8,128)(2,1)}, u32[]{:S(2)}, u32[]{:S(2)}) async-start(bf16[128,56,256]{2,1,0:T(8,128)(2,1)} %bitcast.3), calls=%async_computation.2 | async-start | bytes 7340032 | tf_op jit(solution)/shard_map/all_to_all | solution.py:485
  101.7 0.2 reshape.29
  101.9 0.2 reshape.30
  102.2 0.7 fusion.30.mirror_ref
  102.9 2.5 %fusion.24.order_ref = bf16[400,448]{1,0:T(8,128)(2,1)} fusion(s32[400]{0:T(512)S(1)} %get-tuple-element.37, s32[400]{0:T(512)S(1)} %get-tuple-element.47, s32[400]{0:T(512)S(1)} %get-tuple-element.38, s32[400]{0:T(512)S(1)} %get-tuple-element.42, s32[400]{0:T(512)S(1)} %get-tuple-element.39, s32[400]{0:T(512)S(1)} %get-tuple-element.48, ...), kind=kLoop, calls=%fused_computation.38 | loop fusion | flops 4659200 | bytes 372800 | tf_op jit(solution)/shard_map/convert_element_type | solution.py:193
  105.4 16.5 %multiply_convert_fusion.1 = (bf16[640,1408]{1,0:T(8,128)(2,1)S(1)}, bf16[640,1408]{1,0:T(8,128)(2,1)S(1)}) fusion(s32[640]{0:T(1024)S(1)} %reshape.30, f32[640]{0:T(1024)S(1)} %get-tuple-element.19, f32[640]{0:T(1024)S(1)} %get-tuple-element.20), kind=kLoop, calls=%fused_computation.10 | loop fusion | flops 11714560 | bytes 3612160 | tf_op jit(solution)/shard_map/convert
  121.9 2.2 %pad_maximum_fusion.table_ref.middle_ref = bf16[1280,1408]{1,0:T(8,128)(2,1)} fusion(bf16[640,1408]{1,0:T(8,128)(2,1)S(1)} %get-tuple-element.18, bf16[640,1408]{1,0:T(8,128)(2,1)S(1)} %get-tuple-element.17), kind=kLoop, calls=%fused_computation.8 | loop fusion | flops 7208960 | bytes 7208960 | tf_op jit(solution)/shard_map/concatenate | solution.py:468
  124.1 25.0 %all-to-all-done.2.u_ref = bf16[128,56,256]{2,1,0:T(8,128)(2,1)} async-done(((bf16[128,56,256]{2,1,0:T(8,128)(2,1)}), bf16[128,56,256]{2,1,0:T(8,128)(2,1)}, u32[]{:S(2)}, u32[]{:S(2)}) %all-to-all-start.2) | async-done | bytes 3670048 | tf_op jit(solution)/shard_map/all_to_all | solution.py:485
  149.1 14.0 %fourier.1 = bf16[5,256,2560]{2,1,0:T(8,128)(2,1)} custom-call(bf16[128,56,256]{2,1,0:T(8,128)(2,1)} %all-to-all-done.2.u_ref, bf16[400,448]{1,0:T(8,128)(2,1)} %fusion.24.order_ref, bf16[256,256]{1,0:T(8,128)(2,1)} %fusion.30.mirror_ref, bf16[1280,1408]{1,0:T(8,128)(2,1)} %pad_maximum_fusion.table_ref.middle_ref, ...), custom_call_target="tpu_custom_call" | custom-call | tf_op jit(solution)/shard_map/fourier/pallas_call | solution.py:437
  (18 shorter events, 0.2 us)
Async XLA Ops:
  7.9 47.0 %all-to-all-start = ((bf16[32,184,256]{2,1,0:T(8,128)(2,1)}), bf16[32,184,256]{2,1,0:T(8,128)(2,1)S(1)}, u32[]{:S(2)}, u32[]{:S(2)}) async-start(bf16[32,184,256]{2,1,0:T(8,128)(2,1)} %pack_first.1), calls=%async_computation | async-start | bytes 6029312 | tf_op jit(solution)/shard_map/all_to_all | solution.py:474
  16.5 3.8 %copy-start.1 = (s32[640]{0:T(1024)S(1)}, s32[640]{0:T(1024)}, u32[]{:S(2)}) copy-start(s32[640]{0:T(1024)} %param.9) | copy-start | bytes 7684
  54.9 8.8 %copy-start = (bf16[32,184,256]{2,1,0:T(8,128)(2,1)}, bf16[32,184,256]{2,1,0:T(8,128)(2,1)S(1)}, u32[]{:S(2)}) copy-start(bf16[32,184,256]{2,1,0:T(8,128)(2,1)S(1)} %all-to-all-done.rf_ref.rx_ref) | copy-start | bytes 9043972
  54.9 29.1 %all-to-all-start.1 = ((bf16[32,104,256]{2,1,0:T(8,128)(2,1)}), bf16[32,104,256]{2,1,0:T(8,128)(2,1)}, u32[]{:S(2)}, u32[]{:S(2)}) async-start(bf16[32,104,256]{2,1,0:T(8,128)(2,1)} %pack_second.1), calls=%async_computation.1 | async-start | bytes 3407872 | tf_op jit(solution)/shard_map/all_to_all | solution.py:476
  93.8 55.3 %all-to-all-start.2 = ((bf16[128,56,256]{2,1,0:T(8,128)(2,1)}), bf16[128,56,256]{2,1,0:T(8,128)(2,1)}, u32[]{:S(2)}, u32[]{:S(2)}) async-start(bf16[128,56,256]{2,1,0:T(8,128)(2,1)} %bitcast.3), calls=%async_computation.2 | async-start | bytes 7340032 | tf_op jit(solution)/shard_map/all_to_all | solution.py:485
